TPU v7x, 256 devices: a whole 4x4x8 slice. The times are simulated.
256 devices in a mesh: dom: 64 (over y, z, core), lvl: 4 (over x).
Axes of the slice: x: 4, y: 4, z: 8, core: 2. Of those that a mesh axis runs over, the one named last changes fastest.
Arguments:
- displacement: float32 [3, 1048576], P(None, ('dom', 'lvl')), may hold values from -1.8 to 1.8
- velocity: float32 [3, 1048576], P(None, ('dom', 'lvl')), may hold values from -6 to 6
- inverse_mass: float32 [1048576], P(('dom', 'lvl')), may hold values from 0.5 to 2
- levels: int32 [16384], P(('dom', 'lvl')), may hold values from 0 to 3, as said below
- first_lame: float32 [16384], P(('dom', 'lvl')), may hold values from 0.125 to 32
- shear_modulus: float32 [16384], P(('dom', 'lvl')), may hold values from 0.125 to 32
- connectivity: int32 [125, 16384], P(None, ('dom', 'lvl')), may hold values from 0 to 4607, as said below
- owner_list: int32 [131072], P(('dom', 'lvl')), may hold values from 0 to 4095, as said below
Outputs:
- new_displacement: float32 [3, 1048576], P(None, ('dom', 'lvl'))
- new_velocity: float32 [3, 1048576], P(None, ('dom', 'lvl'))
Inputs may be any that keep to these rules, and one draw needn't show every extreme that they name: `levels`: levels 0 to 3. On each device at most 16 elements have level 3, at most 24 level 2 or more, at most 32 level 1 or more; each of these bounds is met on one device of every row of 4 consecutive devices that share a dom index, and every such row holds exactly 32 elements of level 3. `connectivity`: the 125 entries of an element are distinct and form a conforming hexahedral mesh of slabs 2 elements thick chained from device to device in a loop; entries at least 4096 are ghost slots of the next device. `owner_list`: on each device, distinct owned nodes, matching the ghost slots of the previous device.
All inputs are finite; a program needn't handle non-finite values.
Results may differ from a plain program's by a relative error of at most 0.0001.
Values sent between devices are 32-bit elements; how exact they have to be, the bound alone decides.
No kernel may reach another device: no remote copies, remote signals or barrier semaphores. Data moves between devices by JAX's collectives and lax.ppermute only.
A program may use at most 64 MiB of HBM per device.

v0:
```python
import jax
import jax.numpy as jnp
import numpy as np
from jax import lax
from jax.sharding import PartitionSpec as P

substep_length = 0.01


def passed_along(block, axis, distance):
    devices = range(lax.axis_size(axis))
    route = [((i - distance) % len(devices), i) for i in devices]
    return lax.ppermute(block, axis, route)


def lobatto_tables():
    points = np.array([-1.0, -np.sqrt(3.0 / 7.0), 0.0, np.sqrt(3.0 / 7.0), 1.0])
    weights = np.array([0.1, 49.0 / 90.0, 32.0 / 45.0, 49.0 / 90.0, 0.1])
    factor = np.array(
        [np.prod([points[i] - points[k] for k in range(5) if k != i]) for i in range(5)]
    )
    matrix = np.zeros((5, 5))
    for i in range(5):
        for j in range(5):
            if i == j:
                matrix[i, j] = sum((1.0 / (points[i] - points[k]) for k in range(5) if k != i))
            else:
                matrix[i, j] = factor[i] / (factor[j] * (points[i] - points[j]))
    cube = weights[:, None, None] * weights[None, :, None] * weights[None, None, :]
    return (jnp.asarray(matrix, jnp.float32), jnp.asarray(cube, jnp.float32))


def element_force(values, lame_first, lame_shear, tables):
    derivative, weight_cube = tables
    highest = lax.Precision.HIGHEST
    field = values.reshape(3, 5, 5, 5, -1)
    along_first = jnp.einsum("pi,cijkb->cpjkb", derivative, field, precision=highest)
    along_second = jnp.einsum("qj,cijkb->ciqkb", derivative, field, precision=highest)
    along_third = jnp.einsum("rk,cijkb->cijrb", derivative, field, precision=highest)
    gradient = jnp.stack([along_first, along_second, along_third], axis=1)
    divergence = along_first[0] + along_second[1] + along_third[2]
    unit_matrix = jnp.eye(3, dtype=jnp.float32)
    stress = (
        lame_shear * (gradient + jnp.swapaxes(gradient, 0, 1))
        + lame_first * divergence[None, None] * unit_matrix[:, :, None, None, None, None]
    )
    weighted = stress * weight_cube[None, None, :, :, :, None]
    forces = jnp.einsum("pi,cpjkb->cijkb", derivative, weighted[:, 0], precision=highest)
    forces = forces + jnp.einsum("qj,ciqkb->cijkb", derivative, weighted[:, 1], precision=highest)
    forces = forces + jnp.einsum("rk,cijrb->cijkb", derivative, weighted[:, 2], precision=highest)
    return forces.reshape(3, 125, -1)


def select_members(levels, threshold, capacity):
    element_count = levels.shape[0]
    member_mask = levels >= threshold
    position = jnp.cumsum(member_mask.astype(jnp.int32)) - 1
    target_spot = jnp.where(member_mask, position, capacity)
    chosen = (
        jnp.zeros((capacity,), jnp.int32)
        .at[target_spot]
        .set(jnp.arange(element_count, dtype=jnp.int32), mode="drop")
    )
    usable = (
        jnp.arange(capacity, dtype=jnp.int32) < jnp.sum(member_mask.astype(jnp.int32))
    ).astype(jnp.float32)
    return (chosen, usable)


def home_forces(
    extended, chosen, usable, period_value, connectivity, first_lame, shear_modulus, tables
):
    nodes_of = connectivity[:, chosen]
    forces = element_force(extended[:, nodes_of], first_lame[chosen], shear_modulus[chosen], tables)
    forces = forces * (period_value[chosen] * usable)[None, None, :]
    return (nodes_of, forces)


def per_device(
    displacement,
    velocity,
    inverse_mass,
    levels,
    first_lame,
    shear_modulus,
    connectivity,
    owner_list,
):
    tables = lobatto_tables()
    owned_nodes = displacement.shape[1]
    ghost_count = owner_list.shape[0]
    element_count = levels.shape[0]
    fine_most = element_count // 4
    mid_most = 3 * element_count // 8
    coarse_most = element_count // 2
    period = jnp.where(
        levels == 0, 8, jnp.where(levels == 1, 4, jnp.where(levels == 2, 2, 1))
    ).astype(jnp.int32)
    period_value = period.astype(jnp.float32)
    everyone = jnp.arange(element_count, dtype=jnp.int32)
    every_usable = jnp.ones((element_count,), jnp.float32)
    coarse_set = select_members(levels, 1, coarse_most)
    mid_set = select_members(levels, 2, mid_most)
    fine_set = select_members(levels, 3, fine_most)
    for substep in range(8):
        ghost_values = passed_along(displacement[:, owner_list], ("dom", "lvl"), -1)
        extended = jnp.concatenate([displacement, ghost_values], axis=1)
        if substep == 0:
            nodes_of, forces = home_forces(
                extended,
                everyone,
                every_usable,
                period_value,
                connectivity,
                first_lame,
                shear_modulus,
                tables,
            )
        elif substep % 2 == 1:
            nodes_of, forces = home_forces(
                extended,
                fine_set[0],
                fine_set[1],
                period_value,
                connectivity,
                first_lame,
                shear_modulus,
                tables,
            )
        elif substep == 4:
            nodes_of, forces = home_forces(
                extended,
                coarse_set[0],
                coarse_set[1],
                period_value,
                connectivity,
                first_lame,
                shear_modulus,
                tables,
            )
        else:
            nodes_of, forces = home_forces(
                extended,
                mid_set[0],
                mid_set[1],
                period_value,
                connectivity,
                first_lame,
                shear_modulus,
                tables,
            )
        assembled = (
            jnp.zeros((3, owned_nodes + ghost_count), jnp.float32).at[:, nodes_of].add(forces)
        )
        partials = passed_along(assembled[:, owned_nodes:], ("dom", "lvl"), 1)
        node_force = assembled[:, :owned_nodes].at[:, owner_list].add(partials)
        velocity = velocity - substep_length * inverse_mass[None, :] * node_force
        displacement = displacement + substep_length * velocity
    return (displacement, velocity)


def solution(mesh):
    in_specs = (
        P(None, ("dom", "lvl")),
        P(None, ("dom", "lvl")),
        P(("dom", "lvl")),
        P(("dom", "lvl")),
        P(("dom", "lvl")),
        P(("dom", "lvl")),
        P(None, ("dom", "lvl")),
        P(("dom", "lvl")),
    )
    out_specs = (P(None, ("dom", "lvl")), P(None, ("dom", "lvl")))
    return jax.shard_map(
        per_device, mesh=mesh, in_specs=in_specs, out_specs=out_specs, check_vma=False
    )
```

profile of v0, /device:TPU:0, one launch (start us, length us, event | category | flops | bytes accessed | tf_op | source)
XLA Modules:
  0.0 530.9 jit_solution(1825216856806816842)
XLA Ops:
  3.9 8.3 %collective-permute-start = (f32[3,512]{0,1:T(8,128)S(1)}, f32[3,512]{0,1:T(8,128)S(1)}, u32[]{:S(2)}, u32[]{:S(2)}) collective-permute-start(f32[3,512]{0,1:T(8,128)S(1)} %bitcast.624), channel_id=1, source_target_pairs={{1,0},{2,1},{3,2},{4,3},{5,4},{6,5},{7,6},{8,7},{9,8},{10,9},{11,1... | collective-permute-start | bytes 18440 | tf_op jit(solution)/shard_map/ppermute | solution.py:13
  23.9 17.5 %gather_fusion.3 = f32[8000,3]{1,0:T(8,128)} fusion(f32[3,4608]{0,1:T(8,128)} %pad_maximum_fusion, s32[8192]{0:T(1024)S(1)} %pad_clamp_fusion), kind=kCustom, calls=%fused_computation.3 | custom fusion | bytes 224000 | tf_op jit(solution)/shard_map/gather | solution.py:74
  50.5 45.0 %scatter_custom_fusion = f32[3,4608]{0,1:T(8,128)S(1)} fusion(s32[8000]{0:T(1024)S(1)} %reshape.652, f32[8000,3]{1,0:T(8,128)} %bitcast.546, f32[]{:T(128)} %constant.18.clone.1), kind=kCustom, calls=%fused_computation.90 | custom fusion | flops 24000 | bytes 55808 | tf_op jit(solution)/shard_map/scatter-add | solution.py:153
  98.2 8.9 %collective-permute-done.1 = f32[3,512]{0,1:T(8,128)S(1)} collective-permute-done((f32[3,512]{0,1:T(8,128)S(1)}, f32[3,512]{0,1:T(8,128)S(1)}, u32[]{:S(2)}, u32[]{:S(2)}) %collective-permute-start.1) | collective-permute-done | bytes 6176 | tf_op jit(solution)/shard_map/ppermute | solution.py:13
  121.6 7.6 %gather_fusion.9 = f32[2000,3]{1,0:T(8,128)} fusion(f32[3,4608]{0,1:T(8,128)S(1)} %copy.827, s32[2048]{0:T(1024)S(1)} %pad_clamp_fusion.3), kind=kCustom, calls=%fused_computation.9 | custom fusion | bytes 56000 | tf_op jit(solution)/shard_map/gather | solution.py:74
  136.5 14.4 %scatter_custom_fusion.3 = f32[3,4608]{0,1:T(8,128)S(1)} fusion(s32[2000]{0:T(1024)S(1)} %reshape.676, f32[2000,3]{1,0:T(8,128)} %bitcast.606, f32[]{:T(128)} %constant.18.clone.1), kind=kCustom, calls=%fused_computation.88 | custom fusion | flops 6000 | bytes 55808 | tf_op jit(solution)/shard_map/scatter-add | solution.py:153
  153.9 8.8 %collective-permute-done.3 = f32[3,512]{0,1:T(8,128)S(1)} collective-permute-done((f32[3,512]{0,1:T(8,128)S(1)}, f32[3,512]{0,1:T(8,128)S(1)}, u32[]{:S(2)}, u32[]{:S(2)}) %collective-permute-start.3) | collective-permute-done | bytes 6176 | tf_op jit(solution)/shard_map/ppermute | solution.py:13
  162.7 6.1 %scatter_custom_fusion.4 = f32[3,4096]{0,1:T(8,128)} fusion(f32[3,4096]{0,1:T(8,128)} %slice.334, s32[512]{0:T(512)} %copy-done.39, f32[3,512]{0,1:T(8,128)S(1)} %collective-permute-done.3), kind=kCustom, calls=%fused_computation.264 | custom fusion | flops 1536 | bytes 55296 | tf_op jit(solution)/shard_map/scatter-add | solution.py:156
  178.0 10.9 %gather_fusion.15 = f32[3000,3]{1,0:T(8,128)} fusion(f32[3,4608]{0,1:T(8,128)S(1)} %copy.848, s32[3072]{0:T(1024)S(1)} %pad_clamp_fusion.2), kind=kCustom, calls=%fused_computation.15 | custom fusion | bytes 84000 | tf_op jit(solution)/shard_map/gather | solution.py:74
  196.5 19.1 %scatter_custom_fusion.6 = f32[3,4608]{0,1:T(8,128)S(1)} fusion(s32[3000]{0:T(1024)S(1)} %reshape.700, f32[3000,3]{1,0:T(8,128)} %bitcast.600, f32[]{:T(128)} %constant.18.clone.1), kind=kCustom, calls=%fused_computation.86 | custom fusion | flops 9000 | bytes 55808 | tf_op jit(solution)/shard_map/scatter-add | solution.py:153
  218.0 9.1 %collective-permute-done.5 = f32[3,512]{0,1:T(8,128)S(1)} collective-permute-done((f32[3,512]{0,1:T(8,128)S(1)}, f32[3,512]{0,1:T(8,128)S(1)}, u32[]{:S(2)}, u32[]{:S(2)}) %collective-permute-start.5) | collective-permute-done | bytes 6176 | tf_op jit(solution)/shard_map/ppermute | solution.py:13
  252.5 14.4 %scatter_custom_fusion.8 = f32[3,4608]{0,1:T(8,128)S(1)} fusion(s32[2000]{0:T(1024)} %copy-done.28, f32[2000,3]{1,0:T(8,128)S(1)} %bitcast.607, f32[]{:T(128)} %constant.18.clone.1), kind=kCustom, calls=%fused_computation.84 | custom fusion | flops 6000 | bytes 55808 | tf_op jit(solution)/shard_map/scatter-add | solution.py:153
  270.2 8.2 %collective-permute-done.7 = f32[3,512]{0,1:T(8,128)S(1)} collective-permute-done((f32[3,512]{0,1:T(8,128)S(1)}, f32[3,512]{0,1:T(8,128)S(1)}, u32[]{:S(2)}, u32[]{:S(2)}) %collective-permute-start.7) | collective-permute-done | bytes 6176 | tf_op jit(solution)/shard_map/ppermute | solution.py:13
  293.1 14.2 %gather_fusion.23 = f32[4000,3]{1,0:T(8,128)} fusion(f32[3,4608]{0,1:T(8,128)S(1)} %copy.890, s32[4096]{0:T(1024)S(1)} %pad_clamp_fusion.1), kind=kCustom, calls=%fused_computation.23 | custom fusion | bytes 112000 | tf_op jit(solution)/shard_map/gather | solution.py:74
  315.2 24.2 %scatter_custom_fusion.11 = f32[3,4608]{0,1:T(8,128)S(1)} fusion(s32[4000]{0:T(1024)S(1)} %reshape.740, f32[4000,3]{1,0:T(8,128)} %bitcast.548, f32[]{:T(128)} %constant.18.clone.1), kind=kCustom, calls=%fused_computation.82 | custom fusion | flops 12000 | bytes 55808 | tf_op jit(solution)/shard_map/scatter-add | solution.py:153
  341.5 9.7 %collective-permute-done.9 = f32[3,512]{0,1:T(8,128)S(1)} collective-permute-done((f32[3,512]{0,1:T(8,128)S(1)}, f32[3,512]{0,1:T(8,128)S(1)}, u32[]{:S(2)}, u32[]{:S(2)}) %collective-permute-start.9) | collective-permute-done | bytes 6176 | tf_op jit(solution)/shard_map/ppermute | solution.py:13
  365.8 7.6 %gather_fusion.27 = f32[2000,3]{1,0:T(8,128)} fusion(f32[3,4608]{0,1:T(8,128)S(1)} %copy.909, s32[2048]{0:T(1024)S(1)} %pad_clamp_fusion.3), kind=kCustom, calls=%fused_computation.27 | custom fusion | bytes 56000 | tf_op jit(solution)/shard_map/gather | solution.py:74
  380.7 14.4 %scatter_custom_fusion.13 = f32[3,4608]{0,1:T(8,128)S(1)} fusion(s32[2000]{0:T(1024)} %copy-done.28, f32[2000,3]{1,0:T(8,128)} %bitcast.608, f32[]{:T(128)} %constant.18.clone.1), kind=kCustom, calls=%fused_computation.80 | custom fusion | flops 6000 | bytes 55808 | tf_op jit(solution)/shard_map/scatter-add | solution.py:153
  396.9 9.7 %collective-permute-done.11 = f32[3,512]{0,1:T(8,128)S(1)} collective-permute-done((f32[3,512]{0,1:T(8,128)S(1)}, f32[3,512]{0,1:T(8,128)S(1)}, u32[]{:S(2)}, u32[]{:S(2)}) %collective-permute-start.11) | collective-permute-done | bytes 6176 | tf_op jit(solution)/shard_map/ppermute | solution.py:13
  421.3 10.9 %gather_fusion.29 = f32[3000,3]{1,0:T(8,128)} fusion(f32[3,4608]{0,1:T(8,128)S(1)} %copy.930, s32[3072]{0:T(1024)S(1)} %pad_clamp_fusion.2), kind=kCustom, calls=%fused_computation.29 | custom fusion | bytes 84000 | tf_op jit(solution)/shard_map/gather | solution.py:74
  439.8 19.1 %scatter_custom_fusion.15 = f32[3,4608]{0,1:T(8,128)S(1)} fusion(s32[3000]{0:T(1024)} %copy-done.26, f32[3000,3]{1,0:T(8,128)} %bitcast.599, f32[]{:T(128)} %constant.18.clone.1), kind=kCustom, calls=%fused_computation.78 | custom fusion | flops 9000 | bytes 55808 | tf_op jit(solution)/shard_map/scatter-add | solution.py:153
  460.7 9.7 %collective-permute-done.13 = f32[3,512]{0,1:T(8,128)S(1)} collective-permute-done((f32[3,512]{0,1:T(8,128)S(1)}, f32[3,512]{0,1:T(8,128)S(1)}, u32[]{:S(2)}, u32[]{:S(2)}) %collective-permute-start.13) | collective-permute-done | bytes 6176 | tf_op jit(solution)/shard_map/ppermute | solution.py:13
  495.7 14.4 %scatter_custom_fusion.17 = f32[3,4608]{0,1:T(8,128)S(1)} fusion(s32[2000]{0:T(1024)} %copy-done.28, f32[2000,3]{1,0:T(8,128)S(1)} %bitcast.605, f32[]{:T(128)} %constant.18.clone.1), kind=kCustom, calls=%fused_computation.76 | custom fusion | flops 6000 | bytes 55808 | tf_op jit(solution)/shard_map/scatter-add | solution.py:153
  511.8 9.7 %collective-permute-done.15 = f32[3,512]{0,1:T(8,128)S(1)} collective-permute-done((f32[3,512]{0,1:T(8,128)S(1)}, f32[3,512]{0,1:T(8,128)S(1)}, u32[]{:S(2)}, u32[]{:S(2)}) %collective-permute-start.15) | collective-permute-done | bytes 6176 | tf_op jit(solution)/shard_map/ppermute | solution.py:13
  (411 shorter events, 205.7 us)
Async XLA Ops:
  1.4 105.7 %copy-start.39 = (s32[512]{0:T(512)}, s32[512]{0:T(512)S(1)}, u32[]{:S(2)}) copy-start(s32[512]{0:T(512)S(1)} %compare_select_fusion.4) | copy-start | bytes 6148
  1.4 114.6 %copy-start.23 = (s32[1024]{0:T(1024)}, s32[1024]{0:T(1024)S(1)}, u32[]{:S(2)}) copy-start(s32[1024]{0:T(1024)S(1)} %pad_clamp_fusion.7) | copy-start | bytes 12292
  3.9 18.4 %collective-permute-start = (f32[3,512]{0,1:T(8,128)S(1)}, f32[3,512]{0,1:T(8,128)S(1)}, u32[]{:S(2)}, u32[]{:S(2)}) collective-permute-start(f32[3,512]{0,1:T(8,128)S(1)} %bitcast.624), channel_id=1, source_target_pairs={{1,0},{2,1},{3,2},{4,3},{5,4},{6,5},{7,6},{8,7},{9,8},{10,9},{11,1... | collective-permute-start | bytes 18440 | tf_op jit(solution)/shard_map/ppermute | solution.py:13
  16.8 101.7 %copy-start.34 = (s32[1024]{0:T(1024)}, s32[1024]{0:T(1024)S(1)}, u32[]{:S(2)}) copy-start(s32[1024]{0:T(1024)S(1)} %pad_clamp_fusion.5) | copy-start | bytes 12292
  19.3 173.4 %copy-start.21 = (f32[3,3]{0,1:T(4,128)}, f32[3,3]{0,1:T(4,128)S(1)}, u32[]{:S(2)}) copy-start(f32[3,3]{0,1:T(4,128)S(1)} %fusion.152) | copy-start | bytes 112
  95.6 11.5 %collective-permute-start.1 = (f32[3,512]{0,1:T(8,128)S(1)}, f32[3,512]{0,1:T(8,128)S(1)}, u32[]{:S(2)}, u32[]{:S(2)}) collective-permute-start(f32[3,512]{0,1:T(8,128)S(1)} %slice.327), channel_id=1, source_target_pairs={{255,0},{0,1},{1,2},{2,3},{3,4},{4,5},{5,6},{6,7},{7,8},{8,9},{9,1... | collective-permute-start | bytes 18440 | tf_op jit(solution)/shard_map/ppermute | solution.py:13
  117.1 3.7 collective-permute-start.2
  151.0 11.8 %collective-permute-start.3 = (f32[3,512]{0,1:T(8,128)S(1)}, f32[3,512]{0,1:T(8,128)S(1)}, u32[]{:S(2)}, u32[]{:S(2)}) collective-permute-start(f32[3,512]{0,1:T(8,128)S(1)} %slice.335), channel_id=1, source_target_pairs={{255,0},{0,1},{1,2},{2,3},{3,4},{4,5},{5,6},{6,7},{7,8},{8,9},{9,1... | collective-permute-start | bytes 18440 | tf_op jit(solution)/shard_map/ppermute | solution.py:13
  152.2 42.3 %copy-start.44 = (f32[24]{0:T(128)}, f32[24]{0:T(128)S(1)}, u32[]{:S(2)}) copy-start(f32[24]{0:T(128)S(1)} %compare_select_fusion.12) | copy-start | bytes 292
  152.4 44.1 %copy-start.26 = (s32[3000]{0:T(1024)}, s32[3000]{0:T(1024)S(1)}, u32[]{:S(2)}) copy-start(s32[3000]{0:T(1024)S(1)} %reshape.700) | copy-start | bytes 36004
  173.5 3.7 collective-permute-start.4
  215.6 11.5 %collective-permute-start.5 = (f32[3,512]{0,1:T(8,128)S(1)}, f32[3,512]{0,1:T(8,128)S(1)}, u32[]{:S(2)}, u32[]{:S(2)}) collective-permute-start(f32[3,512]{0,1:T(8,128)S(1)} %slice.343), channel_id=1, source_target_pairs={{255,0},{0,1},{1,2},{2,3},{3,4},{4,5},{5,6},{6,7},{7,8},{8,9},{9,1... | collective-permute-start | bytes 18440 | tf_op jit(solution)/shard_map/ppermute | solution.py:13
  237.3 3.7 collective-permute-start.6
  266.9 11.5 %collective-permute-start.7 = (f32[3,512]{0,1:T(8,128)S(1)}, f32[3,512]{0,1:T(8,128)S(1)}, u32[]{:S(2)}, u32[]{:S(2)}) collective-permute-start(f32[3,512]{0,1:T(8,128)S(1)} %slice.351), channel_id=1, source_target_pairs={{255,0},{0,1},{1,2},{2,3},{3,4},{4,5},{5,6},{6,7},{7,8},{8,9},{9,1... | collective-permute-start | bytes 18440 | tf_op jit(solution)/shard_map/ppermute | solution.py:13
  286.8 72.7 %copy-start.10 = (f32[3,4096]{1,0:T(4,128)}, f32[3,4096]{1,0:T(4,128)S(1)}, u32[]{:S(2)}) copy-start(f32[3,4096]{1,0:T(4,128)S(1)} %get-tuple-element.20) | copy-start | bytes 147460
  288.6 3.7 collective-permute-start.8
  339.5 11.7 %collective-permute-start.9 = (f32[3,512]{0,1:T(8,128)S(1)}, f32[3,512]{0,1:T(8,128)S(1)}, u32[]{:S(2)}, u32[]{:S(2)}) collective-permute-start(f32[3,512]{0,1:T(8,128)S(1)} %slice.359), channel_id=1, source_target_pairs={{255,0},{0,1},{1,2},{2,3},{3,4},{4,5},{5,6},{6,7},{7,8},{8,9},{9,1... | collective-permute-start | bytes 18440 | tf_op jit(solution)/shard_map/ppermute | solution.py:13
  361.4 3.7 collective-permute-start.10
  395.2 11.5 %collective-permute-start.11 = (f32[3,512]{0,1:T(8,128)S(1)}, f32[3,512]{0,1:T(8,128)S(1)}, u32[]{:S(2)}, u32[]{:S(2)}) collective-permute-start(f32[3,512]{0,1:T(8,128)S(1)} %slice.367), channel_id=1, source_target_pairs={{255,0},{0,1},{1,2},{2,3},{3,4},{4,5},{5,6},{6,7},{7,8},{8,9},{9,1... | collective-permute-start | bytes 18440 | tf_op jit(solution)/shard_map/ppermute | solution.py:13
  415.0 63.7 %copy-start.8 = (f32[3,4096]{1,0:T(4,128)}, f32[3,4096]{1,0:T(4,128)S(1)}, u32[]{:S(2)}) copy-start(f32[3,4096]{1,0:T(4,128)S(1)} %get-tuple-element.18) | copy-start | bytes 147460
  416.8 3.7 collective-permute-start.12
  458.9 11.5 %collective-permute-start.13 = (f32[3,512]{0,1:T(8,128)S(1)}, f32[3,512]{0,1:T(8,128)S(1)}, u32[]{:S(2)}, u32[]{:S(2)}) collective-permute-start(f32[3,512]{0,1:T(8,128)S(1)} %slice.375), channel_id=1, source_target_pairs={{255,0},{0,1},{1,2},{2,3},{3,4},{4,5},{5,6},{6,7},{7,8},{8,9},{9,1... | collective-permute-start | bytes 18440 | tf_op jit(solution)/shard_map/ppermute | solution.py:13
  480.6 3.7 collective-permute-start.14
  510.2 11.3 %collective-permute-start.15 = (f32[3,512]{0,1:T(8,128)S(1)}, f32[3,512]{0,1:T(8,128)S(1)}, u32[]{:S(2)}, u32[]{:S(2)}) collective-permute-start(f32[3,512]{0,1:T(8,128)S(1)} %slice.383), channel_id=1, source_target_pairs={{255,0},{0,1},{1,2},{2,3},{3,4},{4,5},{5,6},{6,7},{7,8},{8,9},{9,1... | collective-permute-start | bytes 18440 | tf_op jit(solution)/shard_map/ppermute | solution.py:13
  (43 other events, 532.9 us)
where the time goes:
time: 540 us; the launch traced here: 531 us
  other arithmetic  225 us (42%)
  local copies, waits for them, and re-layouts  178 us (33%)
  waiting for transfers between devices  92.4 us (17%)
  matrix products  21.2 us (4%)
  starting transfers between devices  11.3 us (2%)
    scatter-add x8, other arithmetic, per_device(): jnp.zeros((3, owned_nodes + ghost_count), jnp.float32).at[:, nodes_of]  165 us
    gather x16, local copies, waits for them, and re-layouts, home_forces(): extended[:, nodes_of]  95.8 us
    ppermute x16, waiting for transfers between devices, passed_along(): return lax.ppermute(block, axis, route)  92.4 us
    scatter-add x8, other arithmetic, per_device(): node_force = assembled[:, :owned_nodes].at[:, owner_list].add(partials)  48.4 us
    scatter-add x8, local copies, waits for them, and re-layouts, per_device(): node_force = assembled[:, :owned_nodes].at[:, owner_list].add(partials)  17.7 us
    mul x8, local copies, waits for them, and re-layouts, home_forces(): forces = forces * (period_value[chosen] * usable)[None, None, :]  13.9 us
    slice x8, local copies, waits for them, and re-layouts, per_device(): node_force = assembled[:, :owned_nodes].at[:, owner_list].add(partials)  11.9 us
    ppermute x16, starting transfers between devices, passed_along(): return lax.ppermute(block, axis, route)  11.3 us
  transfers between devices with their start and end apart: 16, of which 15 were waited for; matrix products, arithmetic and copies ran while one was open for 6% of the time, Pallas kernels for 0%

commit v1 on v0

v1 whole, which is shorter than its diff:
```python
import jax
import jax.numpy as jnp
import numpy as np
from jax import lax
from jax.experimental import pallas as pl
from jax.experimental.pallas import tpu as pltpu
from jax.sharding import PartitionSpec as P

substep_length = 0.01
AXES = ("dom", "lvl")
SUB, LANE = 8, 128
VALUES = 7
POINTS = 64
ROWS = VALUES * 32 + 16
STAGE = VALUES * POINTS + 16
F32 = jnp.float32


def lobatto():
    points = np.array([-1.0, -np.sqrt(3.0 / 7.0), 0.0, np.sqrt(3.0 / 7.0), 1.0])
    weights = np.array([0.1, 49.0 / 90.0, 32.0 / 45.0, 49.0 / 90.0, 0.1])
    factor = np.array(
        [np.prod([points[i] - points[k] for k in range(5) if k != i]) for i in range(5)]
    )
    matrix = np.zeros((5, 5))
    for i in range(5):
        for j in range(5):
            if i == j:
                matrix[i, j] = sum((1.0 / (points[i] - points[k]) for k in range(5) if k != i))
            else:
                matrix[i, j] = factor[i] / (factor[j] * (points[i] - points[j]))
    return matrix, weights


DER, WEI = lobatto()


def line_derivative(u):
    s0, s1 = u[0] + u[4], u[1] + u[3]
    o0, o1 = u[4] - u[0], u[3] - u[1]
    two = u[2] + u[2]
    e0, e1 = s0 - two, s1 - two
    out = [None] * 5
    for p in range(2):
        even = float((DER[p, 0] + DER[p, 4]) / 2) * e0 + float((DER[p, 1] + DER[p, 3]) / 2) * e1
        odd = float((DER[p, 4] - DER[p, 0]) / 2) * o0 + float((DER[p, 3] - DER[p, 1]) / 2) * o1
        out[p] = odd + even
        out[4 - p] = odd - even
    out[2] = float(DER[2, 4]) * o0 + float(DER[2, 3]) * o1
    return out


def line_transposed(s):
    p0, p1 = s[0] + s[4], s[1] + s[3]
    m0, m1 = s[4] - s[0], s[3] - s[1]
    out = [None] * 5
    for i in range(2):
        minus = float((DER[4, i] - DER[0, i]) / 2) * m0 + float((DER[3, i] - DER[1, i]) / 2) * m1
        plus = (
            float((DER[0, i] + DER[4, i]) / 2) * p0
            + float((DER[1, i] + DER[3, i]) / 2) * p1
            + float(DER[2, i]) * s[2]
        )
        out[i] = minus + plus
        out[4 - i] = minus - plus
    out[2] = float(DER[4, 2]) * m0 + float(DER[3, 2]) * m1
    return out


def lanes(x, index):
    return jnp.take_along_axis(x, index, axis=1, mode="promise_in_bounds")


def as_column(row):
    n = row.shape[1]
    diag = lax.broadcasted_iota(jnp.int32, (n, n), 0) == lax.broadcasted_iota(jnp.int32, (n, n), 1)
    return jnp.sum(jnp.where(diag, jnp.broadcast_to(row, (n, n)), 0.0), axis=1, keepdims=True)


def pack_kernel(u, v, m, lev, lam, mu, conn, own, out, index, stage):
    for i in range(16):
        r = 25 * (i // 4) + 5 * (i % 4)
        stage[4 * i : 4 * i + 4, :] = conn[r : r + 4, :]
    packed = jnp.concatenate([stage[0:32, :], stage[32:64, :]], axis=1)
    index[...] = packed
    for t in range(4):
        part = index[8 * t : 8 * t + 8, :]
        high, low = part >> 7, part & 127
        acc = [jnp.zeros((SUB, LANE), F32) for _ in range(VALUES)]
        for r in range(32):
            here = high == r
            for k in range(VALUES):
                if k < 3:
                    row = u[k : k + 1, r * LANE : (r + 1) * LANE]
                elif k < 6:
                    row = v[k - 3 : k - 2, r * LANE : (r + 1) * LANE]
                else:
                    row = m[r : r + 1, :]
                got = lanes(jnp.broadcast_to(row, (SUB, LANE)), low)
                acc[k] = jnp.where(here, got, acc[k])
        for k in range(VALUES):
            out[k * 32 + 8 * t : k * 32 + 8 * t + 8, :] = acc[k]
    out[VALUES * 32 : ROWS, :] = jnp.zeros((16, LANE), F32)
    corner = {n: conn[r : r + 1, :].astype(F32) for n, r in (("o", 0), ("z", 4), ("y", 20), ("x", 100))}
    column = {n: as_column(c) for n, c in corner.items()}
    n = 64
    which = lax.broadcasted_iota(jnp.int32, (n, n), 0).astype(F32)

    def match(col, row):
        hit = column[col] == corner[row]
        return jnp.sum(jnp.where(hit, which + 1.0, 0.0), axis=0, keepdims=True) - 1.0

    slot = jnp.zeros((n, 1), F32)
    for j in range(4):
        number = (lax.broadcasted_iota(jnp.int32, (n, LANE), 1) + (j * LANE + 1)).astype(F32)
        hit = column["o"] == own[j : j + 1, :].astype(F32)
        slot = slot + jnp.sum(jnp.where(hit, number, 0.0), axis=1, keepdims=True)
    diag = lax.broadcasted_iota(jnp.int32, (n, n), 0) == lax.broadcasted_iota(jnp.int32, (n, n), 1)
    slot_row = jnp.sum(jnp.where(diag, slot, 0.0), axis=0, keepdims=True)
    level = lev[...]
    rows = [
        lam[...],
        mu[...],
        jnp.where(level == 0, 8, jnp.where(level == 1, 4, jnp.where(level == 2, 2, 1))).astype(F32),
        match("o", "z"),
        match("z", "o"),
        match("o", "y"),
        match("y", "o"),
        match("o", "x"),
        match("x", "o"),
        jnp.where(corner["x"] >= 4096.0, corner["x"] - 4096.0, -1.0),
        jnp.where(slot_row > 0.5, slot_row - 1.0, -2.0),
    ]
    for i, row in enumerate(rows):
        out[VALUES * 32 + i : VALUES * 32 + i + 1, 0:64] = row


def place_kernel(index, place):
    acc = jnp.zeros((64, LANE), F32)
    lane = lax.broadcasted_iota(jnp.int32, (32, LANE), 1).astype(F32)
    sub = lax.broadcasted_iota(jnp.int32, (32, LANE), 0)
    wide = lax.broadcasted_iota(jnp.int32, (LANE, LANE), 0)
    for r in range(32):
        row = index[r : r + 1, :]
        here = sub == (row >> 7)
        left = jnp.concatenate(
            [jnp.where(here, float(r), 0.0), jnp.where(here, lane, 0.0)], axis=0
        ).astype(jnp.bfloat16)
        right = jnp.where(wide == (row & 127), 1.0, 0.0).astype(jnp.bfloat16)
        acc = acc + lax.dot_general(
            left, right, (((1,), (1,)), ((), ())), preferred_element_type=F32
        )
    place[...] = acc.astype(jnp.int32)


def pt(c, a, b, k):
    return ((c * 5 + a) * 5 + b) * 5 + k


def main_kernel(
    flags, own, even, odd, r1, r2, r3, s1, s2, s3, place, new_u, new_v,
    stage, disp, gy, gz, force, tab, table,
):
    def at(ref, row):
        if isinstance(row, int):
            return ref[row * SUB : row * SUB + SUB, :]
        return ref[pl.ds(pl.multiple_of(row * SUB, SUB), SUB), :]

    def put(ref, row, value):
        if isinstance(row, int):
            ref[row * SUB : row * SUB + SUB, :] = value
        else:
            ref[pl.ds(pl.multiple_of(row * SUB, SUB), SUB), :] = value

    parity, me = flags[0], flags[1]
    lane = lax.broadcasted_iota(jnp.int32, (SUB, LANE), 1)
    sub = lax.broadcasted_iota(jnp.int32, (SUB, LANE), 0)
    right_half = lane >= 64
    is_odd = jnp.full((SUB, LANE), parity, jnp.int32) == 1
    base = VALUES * POINTS

    def spread(get, position):
        for r in range(0, VALUES * 32, SUB):
            x = get(r)
            k, q = r // 32, r % 32
            stage[pl.ds((k * POINTS + q) * SUB + position, SUB, stride=SUB), :] = x
            stage[pl.ds((k * POINTS + q + 32) * SUB + position, SUB, stride=SUB), :] = pltpu.roll(x, 64, 1)
        for r in range(0, 16, SUB):
            stage[pl.ds((base + r) * SUB + position, SUB, stride=SUB), :] = get(VALUES * 32 + r)

    spread(lambda r: own[r : r + SUB, :], 4)
    spread(lambda r: jnp.where(is_odd, even[r : r + SUB, :], odd[r : r + SUB, :]), 0)
    for other, near, cross in ((1, r1, s1), (2, r2, s2), (3, r3, s3)):
        partner = lax.bitwise_xor(me, other)
        away = partner - me
        spread(lambda r, near=near: near[r : r + SUB, :], 4 + away)
        spread(lambda r, cross=cross: cross[r : r + SUB, :], jnp.where(away > 0, away, away + 8))
    last = sub == 7
    for r in range(0, ROWS, SUB):
        x = jnp.where(is_odd, odd[r : r + SUB, :], even[r : r + SUB, :])
        y = pltpu.roll(x, 64, 1)
        if r < VALUES * 32:
            k, q = r // 32, r % 32
            pairs = ((k * POINTS + q, y), (k * POINTS + q + 32, x))
        else:
            pairs = ((base + r - VALUES * 32, y),)
        for row, value in pairs:
            where = pl.ds(row * SUB + 7, SUB, stride=SUB)
            stage[where, :] = jnp.where(right_half, value, stage[where, :])

    elem = [at(stage, base + i) for i in range(11)]
    lame, shear = elem[0], elem[1]
    period = elem[2].astype(jnp.int32)
    half = jnp.where(right_half, 64, 0)
    next_z = jnp.maximum(elem[3], 0.0).astype(jnp.int32) + half
    prev_z = jnp.maximum(elem[4], 0.0).astype(jnp.int32) + half
    next_y = jnp.maximum(elem[5], 0.0).astype(jnp.int32) + half
    prev_y = jnp.maximum(elem[6], 0.0).astype(jnp.int32) + half
    ghost = elem[9]
    corner = elem[10]
    corner_next = jnp.where(last, pltpu.roll(corner, 64, 1), pltpu.roll(corner, 7, 0))
    ghost_t, corner_t = ghost.T, corner_next.T
    number = lax.broadcasted_iota(jnp.int32, (64, LANE), 0).astype(F32)
    to_next = jnp.zeros((SUB, LANE), F32)
    to_prev = jnp.zeros((SUB, LANE), F32)
    for s in range(SUB):
        hit = corner_t[0:64, s : s + 1] == ghost[s : s + 1, :]
        found = jnp.sum(jnp.where(hit, number, 0.0), axis=0, keepdims=True)
        to_next = jnp.where(sub == s, found, to_next)
        hit = ghost_t[0:64, s : s + 1] == corner_next[s : s + 1, :]
        found = jnp.sum(jnp.where(hit, number, 0.0), axis=0, keepdims=True)
        to_prev = jnp.where(sub == s, found, to_prev)
    to_next = to_next.astype(jnp.int32)
    to_prev = to_prev.astype(jnp.int32)
    inner = elem[7] >= 0.0
    tail = last & right_half
    next_x = jnp.where(
        inner, elem[7].astype(jnp.int32) + half, jnp.where(tail, lane, jnp.where(last, to_next + 64, to_next))
    )
    next_cross = jnp.logical_not(inner | last)
    inner = elem[8] >= 0.0
    from_prev = jnp.where(tail, pltpu.roll(to_prev, 64, 1), pltpu.roll(to_prev, 1, 0))
    prev_x = jnp.where(inner, elem[8].astype(jnp.int32) + half, from_prev)
    prev_cross = jnp.logical_not(inner | tail)
    no_prev = (sub == 0) & jnp.logical_not(inner)
    step = jnp.float32(substep_length)

    for c in range(3):
        for p in range(POINTS):
            a, b, k = p // 16, p // 4 % 4, p % 4
            put(disp, pt(c, a, b, k), at(stage, c * POINTS + p))
    for p in range(POINTS):
        put(stage, 6 * POINTS + p, step * at(stage, 6 * POINTS + p))

    def one_substep(s, carry):
        weight = jnp.where((s & (period - 1)) == 0, period, 0).astype(F32)
        lame_s, shear_s = lame * weight, shear * weight
        for b in range(5):
            for k in range(5):
                w = float(WEI[b] * WEI[k])
                put(tab, b * 5 + k, lame_s * w)
                put(tab, 25 + b * 5 + k, shear_s * w)

        def expand(c, carry):
            o = c * 125
            for a in range(4):
                for b in range(4):
                    put(disp, o + pt(0, a, b, 4), lanes(at(disp, o + pt(0, a, b, 0)), next_z))
            for a in range(4):
                for k in range(5):
                    put(disp, o + pt(0, a, 4, k), lanes(at(disp, o + pt(0, a, 0, k)), next_y))
            for b in range(5):
                for k in range(5):
                    x = at(disp, o + pt(0, 0, b, k))
                    value = jnp.where(next_cross, lanes(pltpu.roll(x, 7, 0), next_x), lanes(x, next_x))
                    put(disp, o + pt(0, 4, b, k), value)
            return carry

        lax.fori_loop(0, 3, expand, 0)

        def planes(j, carry):
            o = j * 25
            plane = [[at(disp, o + b * 5 + k) for k in range(5)] for b in range(5)]
            for b in range(5):
                for k, value in enumerate(line_derivative(plane[b])):
                    put(gz, o + b * 5 + k, value)
            for k in range(5):
                for b, value in enumerate(line_derivative([plane[b][k] for b in range(5)])):
                    put(gy, o + b * 5 + k, value)
            return carry

        lax.fori_loop(0, 15, planes, 0)

        def stresses(b, carry):
            for k in range(5):
                gx = [
                    line_derivative([at(disp, b * 5 + pt(c, a, 0, k)) for a in range(5)])
                    for c in range(3)
                ]
                lw, mw = at(tab, b * 5 + k), at(tab, 25 + b * 5 + k)
                scaled = [(float(WEI[a]) * lw, float(WEI[a]) * mw) for a in range(3)]
                scaled = [(x, y, y + y) for x, y in scaled]
                sx = [[None] * 5 for _ in range(3)]
                for a in range(5):
                    la, ma, m2 = scaled[min(a, 4 - a)]
                    rows = [b * 5 + pt(c, a, 0, k) for c in range(3)]
                    y = [at(gy, r) for r in rows]
                    z = [at(gz, r) for r in rows]
                    xx, yx, zx = gx[0][a], gx[1][a], gx[2][a]
                    spread_of = la * (xx + y[1] + z[2])
                    sx[0][a] = m2 * xx + spread_of
                    sx[1][a] = ma * (yx + y[0])
                    sx[2][a] = ma * (zx + z[0])
                    yz = ma * (y[2] + z[1])
                    put(gy, rows[0], sx[1][a])
                    put(gy, rows[1], m2 * y[1] + spread_of)
                    put(gy, rows[2], yz)
                    put(gz, rows[0], sx[2][a])
                    put(gz, rows[1], yz)
                    put(gz, rows[2], m2 * z[2] + spread_of)
                for c in range(3):
                    for a, value in enumerate(line_transposed(sx[c])):
                        put(force, b * 5 + pt(c, a, 0, k), value)
            return carry

        lax.fori_loop(0, 5, stresses, 0)

        def gather_planes(j, carry):
            o = j * 25
            total = [[at(force, o + b * 5 + k) for k in range(5)] for b in range(5)]
            for b in range(5):
                for k, value in enumerate(line_transposed([at(gz, o + b * 5 + k) for k in range(5)])):
                    total[b][k] = total[b][k] + value
            for k in range(5):
                for b, value in enumerate(line_transposed([at(gy, o + b * 5 + k) for b in range(5)])):
                    total[b][k] = total[b][k] + value
            for b in range(5):
                for k in range(5):
                    put(force, o + b * 5 + k, total[b][k])
            return carry

        lax.fori_loop(0, 15, gather_planes, 0)

        def fold(c, carry):
            o = c * 125
            for b in range(5):
                for k in range(5):
                    x = at(force, o + pt(0, 4, b, k))
                    value = jnp.where(prev_cross, lanes(pltpu.roll(x, 1, 0), prev_x), lanes(x, prev_x))
                    row = o + pt(0, 0, b, k)
                    put(force, row, at(force, row) + jnp.where(no_prev, 0.0, value))
            for a in range(4):
                for k in range(5):
                    row = o + pt(0, a, 0, k)
                    put(force, row, at(force, row) + lanes(at(force, o + pt(0, a, 4, k)), prev_y))
            for p in range(POINTS):
                a, b, k = p // 16, p // 4 % 4, p % 4
                row = o + pt(0, a, b, k)
                f = at(force, row)
                if k == 0:
                    f = f + lanes(at(force, o + pt(0, a, b, 4)), prev_z)
                vrow = (3 + c) * POINTS + p
                vel = at(stage, vrow) - at(stage, 6 * POINTS + p) * f
                put(stage, vrow, vel)
                put(disp, row, at(disp, row) + step * vel)
            return carry

        lax.fori_loop(0, 3, fold, 0)
        return carry

    lax.fori_loop(0, 8, one_substep, 0)

    left4 = lax.broadcasted_iota(jnp.int32, (4, LANE), 1) < 64
    for c in range(3):
        for q in range(0, 32, 4):
            a, b = q // 16, q // 4 % 4
            x = disp[pl.ds(pt(c, a, b, 0) * SUB + 4, 4, stride=SUB), :]
            y = disp[pl.ds(pt(c, a + 2, b, 0) * SUB + 4, 4, stride=SUB), :]
            table[c * 32 + q : c * 32 + q + 4, :] = jnp.where(left4, x, pltpu.roll(y, 64, 1))
        for q in range(0, 32, SUB):
            x = stage[pl.ds(((3 + c) * POINTS + q) * SUB + 4, SUB, stride=SUB), :]
            y = stage[pl.ds(((3 + c) * POINTS + q + 32) * SUB + 4, SUB, stride=SUB), :]
            table[(3 + c) * 32 + q : (3 + c) * 32 + q + SUB, :] = jnp.where(
                right_half, pltpu.roll(y, 64, 1), x
            )
    for t in range(4):
        high, low = place[8 * t : 8 * t + 8, :], place[32 + 8 * t : 32 + 8 * t + 8, :]
        acc = [jnp.zeros((SUB, LANE), F32) for _ in range(6)]
        for q in range(32):
            here = high == q
            for k in range(6):
                row = table[k * 32 + q : k * 32 + q + 1, :]
                acc[k] = jnp.where(here, lanes(jnp.broadcast_to(row, (SUB, LANE)), low), acc[k])
        for k in range(6):
            for j in range(SUB):
                n = (8 * t + j) * LANE
                ref = new_u if k < 3 else new_v
                ref[k % 3 : k % 3 + 1, n : n + LANE] = acc[k][j : j + 1, :]


VMEM = pl.BlockSpec(memory_space=pltpu.VMEM)
SMEM = pl.BlockSpec(memory_space=pltpu.SMEM)


def per_device(displacement, velocity, inverse_mass, levels, first_lame, shear_modulus, connectivity, owner_list):
    rows, across = lax.axis_size("dom"), lax.axis_size("lvl")
    block, index = pl.pallas_call(
        pack_kernel,
        out_shape=(
            jax.ShapeDtypeStruct((ROWS, LANE), F32),
            jax.ShapeDtypeStruct((32, LANE), jnp.int32),
        ),
        in_specs=[VMEM] * 8,
        out_specs=(VMEM, VMEM),
        scratch_shapes=[pltpu.VMEM((64, 64), jnp.int32)],
        name="pack",
    )(
        displacement,
        velocity,
        inverse_mass.reshape(32, LANE),
        levels.reshape(1, 64),
        first_lame.reshape(1, 64),
        shear_modulus.reshape(1, 64),
        connectivity,
        owner_list.reshape(4, LANE),
    )

    def swap_rows(x, shift):
        pairs = []
        for r in range(rows):
            partner = (r ^ 1) if shift == 0 else (((r - 1) ^ 1) + 1) % rows
            pairs += [(r * across + i, partner * across + i) for i in range(across)]
        return lax.ppermute(x, AXES, pairs)

    def swap_near(x, other):
        pairs = [(r * across + i, r * across + (i ^ other)) for r in range(rows) for i in range(across)]
        return lax.ppermute(x, AXES, pairs)

    even = swap_rows(block, 0)
    odd = swap_rows(block, 1)
    near = [swap_near(block, other) for other in (1, 2, 3)]
    place = pl.pallas_call(
        place_kernel,
        out_shape=jax.ShapeDtypeStruct((64, LANE), jnp.int32),
        in_specs=[VMEM],
        out_specs=VMEM,
        name="place",
        cost_estimate=pl.CostEstimate(flops=67_000_000, bytes_accessed=50_000, transcendentals=0),
    )(index)
    parity = lax.axis_index("dom") % 2
    me = lax.axis_index("lvl")
    give_prev_1 = me % 2 == 1
    give_prev_2 = me >= 2
    prev_is_even = parity == 1
    send_1 = jnp.where(give_prev_1 == prev_is_even, even, odd)
    send_2 = jnp.where(give_prev_2 == prev_is_even, even, odd)
    cross = [swap_near(send_1, 1), swap_near(send_2, 2), swap_near(send_2, 3)]
    flags = jnp.stack([parity, me]).astype(jnp.int32)
    return pl.pallas_call(
        main_kernel,
        out_shape=(
            jax.ShapeDtypeStruct((3, 4096), F32),
            jax.ShapeDtypeStruct((3, 4096), F32),
        ),
        in_specs=[SMEM] + [VMEM] * 10,
        out_specs=(VMEM, VMEM),
        scratch_shapes=[
            pltpu.VMEM((STAGE * SUB, LANE), F32),
            pltpu.VMEM((375 * SUB, LANE), F32),
            pltpu.VMEM((375 * SUB, LANE), F32),
            pltpu.VMEM((375 * SUB, LANE), F32),
            pltpu.VMEM((375 * SUB, LANE), F32),
            pltpu.VMEM((50 * SUB, LANE), F32),
            pltpu.VMEM((6 * 32, LANE), F32),
        ],
        compiler_params=pltpu.CompilerParams(vmem_limit_bytes=40 * 1024 * 1024),
        name="substeps",
    )(flags, block, even, odd, *near, *cross, place)


def solution(mesh):
    both = P(None, AXES)
    flat = P(AXES)
    in_specs = (both, both, flat, flat, flat, flat, both, flat)
    return jax.shard_map(
        per_device, mesh=mesh, in_specs=in_specs, out_specs=(both, both), check_vma=False
    )
```

time: 540 us -> 72.9 us (0.14)
  the two profiles are of different devices: /device:TPU:0 before, /device:TPU:1 now
where the time goes in v1:
time: 72.9 us; the launch traced here: 72.6 us
  Pallas kernels  45.9 us (63%)
  starting transfers between devices  17.9 us (25%)
  waiting for transfers between devices  5.85 us (8%)
  local copies, waits for them, and re-layouts  2.25 us (3%)
    pallas_call x1, Pallas kernels, per_device(): pl.pallas_call(main_kernel, out_shape=(jax.ShapeDtypeStruct((3, 4096), F3...  40.9 us
    ppermute x2, starting transfers between devices, swap_rows(): return lax.ppermute(x, AXES, pairs)  9.25 us
    ppermute x6, starting transfers between devices, swap_near(): return lax.ppermute(x, AXES, pairs)  8.6 us
    ppermute x6, waiting for transfers between devices, swap_near(): return lax.ppermute(x, AXES, pairs)  5.84 us
    pallas_call x1, Pallas kernels, per_device(): pl.pallas_call(pack_kernel, out_shape=(jax.ShapeDtypeStruct((ROWS, LANE),...  2.87 us
    unnamed x5, local copies, waits for them, and re-layouts  2.25 us
    pallas_call x1, Pallas kernels, per_device(): pl.pallas_call(place_kernel, out_shape=jax.ShapeDtypeStruct((64, LANE), j...  2.16 us
  transfers between devices with their start and end apart: 8, of which 2 were waited for; matrix products, arithmetic and copies ran while one was open for 0% of the time, Pallas kernels for 3%

profile of v1, /device:TPU:1, one launch (start us, length us, event | category | flops | bytes accessed | tf_op | source)
XLA Modules:
  0.0 72.6 jit_solution(242795943355925201)
XLA Ops:
  0.6 1.5 %copy.10.conn = s32[125,64]{1,0:T(8,128)} copy(s32[125,64]{0,1:T(8,128)} %param.14) | data formatting | bytes 64000 | tf_op args[6]
  2.1 2.9 %pack.1 = (f32[240,128]{1,0:T(8,128)}, s32[32,128]{1,0:T(8,128)}) custom-call(f32[3,4096]{1,0:T(4,128)} %u.1, f32[3,4096]{1,0:T(4,128)} %v.1, f32[32,128]{1,0:T(8,128)} %bitcast.7, s32[1,64]{1,0:T(1,128)} %bitcast.9, f32[1,64]{1,0:T(1,128)} %bitcast.10, f32[1,64]{1,0:T(1,128)} %bitcast.11, s32[125,64]{1,0:T(8,128)} %copy.10.conn, s32[4,128]{1,0:T(4,128)} %bitcast.8), custom_call_target="tpu_custom_call" | custom-call | tf_op jit(solution)/shard_map/pack/pallas_call | solution.py:407
  5.0 3.0 %collective-permute-start.1 = (f32[240,128]{1,0:T(8,128)}, f32[240,128]{1,0:T(8,128)S(1)}, u32[]{:S(2)}, u32[]{:S(2)}) collective-permute-start(f32[240,128]{1,0:T(8,128)} %get-tuple-element.4.own), channel_id=1, source_target_pairs={{0,252},{1,253},{2,254},{3,255},{4,8},{5,9},{6,10},{7,11},{8,4},{9... | collective-permute-start | bytes 368648 | tf_op jit(solution)/shard_map/ppermute | solution.py:433
  8.0 6.2 %collective-permute-start = (f32[240,128]{1,0:T(8,128)}, f32[240,128]{1,0:T(8,128)S(1)}, u32[]{:S(2)}, u32[]{:S(2)}) collective-permute-start(f32[240,128]{1,0:T(8,128)} %get-tuple-element.4.own), channel_id=1, source_target_pairs={{0,4},{1,5},{2,6},{3,7},{4,0},{5,1},{6,2},{7,3},{8,12},{9,13},{10,... | collective-permute-start | bytes 368648 | tf_op jit(solution)/shard_map/ppermute | solution.py:433
  14.2 2.5 %collective-permute-start.4 = (f32[240,128]{1,0:T(8,128)}, f32[240,128]{1,0:T(8,128)S(1)}, u32[]{:S(2)}, u32[]{:S(2)}) collective-permute-start(f32[240,128]{1,0:T(8,128)} %get-tuple-element.4.own), channel_id=1, source_target_pairs={{0,3},{1,2},{2,1},{3,0},{4,7},{5,6},{6,5},{7,4},{8,11},{9,10},{10,... | collective-permute-start | bytes 368648 | tf_op jit(solution)/shard_map/ppermute | solution.py:437
  16.7 0.5 collective-permute-start.3
  17.2 0.3 collective-permute-start.2
  17.5 0.0 collective-permute-done.1.odd
  17.5 0.0 collective-permute-done.even
  17.5 1.3 %collective-permute-start.5 = (f32[240,128]{1,0:T(8,128)S(1)}, f32[240,128]{1,0:T(8,128)S(1)}, u32[]{:S(2)}, u32[]{:S(2)}) collective-permute-start(f32[240,128]{1,0:T(8,128)S(1)} %get-tuple-element.7), channel_id=1, source_target_pairs={{0,1},{1,0},{2,3},{3,2},{4,5},{5,4},{6,7},{7,6},{8,9},{9,8},{10,11... | collective-permute-start | bytes 368648 | tf_op jit(solution)/shard_map/ppermute | solution.py:437
  18.8 1.8 %collective-permute-start.7 = (f32[240,128]{1,0:T(8,128)S(1)}, f32[240,128]{1,0:T(8,128)S(1)}, u32[]{:S(2)}, u32[]{:S(2)}) collective-permute-start(f32[240,128]{1,0:T(8,128)S(1)} %get-tuple-element.6), channel_id=1, source_target_pairs={{0,3},{1,2},{2,1},{3,0},{4,7},{5,6},{6,5},{7,4},{8,11},{9,10},{10,... | collective-permute-start | bytes 368648 | tf_op jit(solution)/shard_map/ppermute | solution.py:437
  20.6 1.6 %collective-permute-done.4.r3 = f32[240,128]{1,0:T(8,128)S(1)} collective-permute-done((f32[240,128]{1,0:T(8,128)}, f32[240,128]{1,0:T(8,128)S(1)}, u32[]{:S(2)}, u32[]{:S(2)}) %collective-permute-start.4) | collective-permute-done | bytes 122912 | tf_op jit(solution)/shard_map/ppermute | solution.py:437
  22.3 2.2 %collective-permute-start.6 = (f32[240,128]{1,0:T(8,128)S(1)}, f32[240,128]{1,0:T(8,128)S(1)}, u32[]{:S(2)}, u32[]{:S(2)}) collective-permute-start(f32[240,128]{1,0:T(8,128)S(1)} %get-tuple-element.6), channel_id=1, source_target_pairs={{0,2},{1,3},{2,0},{3,1},{4,6},{5,7},{6,4},{7,5},{8,10},{9,11},{10,... | collective-permute-start | bytes 368648 | tf_op jit(solution)/shard_map/ppermute | solution.py:437
  24.5 0.0 copy-start
  24.5 2.2 %place.1 = s32[64,128]{1,0:T(8,128)} custom-call(s32[32,128]{1,0:T(8,128)} %get-tuple-element.5.index), custom_call_target="tpu_custom_call" | custom-call | flops 67000000 | bytes 50000 | tf_op jit(solution)/shard_map/place/pallas_call | solution.py:442
  26.7 0.1 pad_add_fusion.flags
  26.8 0.0 collective-permute-done.3.r2
  26.8 0.0 collective-permute-done.2.r1
  26.8 0.0 collective-permute-done.5.s1
  26.8 0.0 collective-permute-done.7.s3
  26.8 4.2 %collective-permute-done.6.s2 = f32[240,128]{1,0:T(8,128)S(1)} collective-permute-done((f32[240,128]{1,0:T(8,128)S(1)}, f32[240,128]{1,0:T(8,128)S(1)}, u32[]{:S(2)}, u32[]{:S(2)}) %collective-permute-start.6) | collective-permute-done | bytes 122912 | tf_op jit(solution)/shard_map/ppermute | solution.py:437
  31.0 0.0 copy-done
  31.0 0.8 %copy-done.1 = s32[64,128]{1,0:T(8,128)S(1)} copy-done((s32[64,128]{1,0:T(8,128)S(1)}, s32[64,128]{1,0:T(8,128)}, u32[]{:S(2)}) %copy-start.1) | copy-done | bytes 32792
  31.7 40.9 %substeps.1 = (f32[3,4096]{1,0:T(4,128)}, f32[3,4096]{1,0:T(4,128)}) custom-call(s32[2]{0:T(128)S(1)} %pad_add_fusion.flags, f32[240,128]{1,0:T(8,128)S(1)} %copy-done, f32[240,128]{1,0:T(8,128)S(1)} %collective-permute-done.even, f32[240,128]{1,0:T(8,128)S(1)} %collective-permute-done.1.odd, f32[240,128]{1,0:T(8,128)S(1)} %collective-permute-done.2.r1, ...), custom_call_target="tpu_custom_call" | custom-call | tf_op jit(solution)/shard_map/substeps/pallas_call | solution.py:459
  (2 shorter events, 0.0 us)
Async XLA Ops:
  5.0 12.5 %collective-permute-start.1 = (f32[240,128]{1,0:T(8,128)}, f32[240,128]{1,0:T(8,128)S(1)}, u32[]{:S(2)}, u32[]{:S(2)}) collective-permute-start(f32[240,128]{1,0:T(8,128)} %get-tuple-element.4.own), channel_id=1, source_target_pairs={{0,252},{1,253},{2,254},{3,255},{4,8},{5,9},{6,10},{7,11},{8,4},{9... | collective-permute-start | bytes 368648 | tf_op jit(solution)/shard_map/ppermute | solution.py:433
  8.0 9.5 %collective-permute-start = (f32[240,128]{1,0:T(8,128)}, f32[240,128]{1,0:T(8,128)S(1)}, u32[]{:S(2)}, u32[]{:S(2)}) collective-permute-start(f32[240,128]{1,0:T(8,128)} %get-tuple-element.4.own), channel_id=1, source_target_pairs={{0,4},{1,5},{2,6},{3,7},{4,0},{5,1},{6,2},{7,3},{8,12},{9,13},{10,... | collective-permute-start | bytes 368648 | tf_op jit(solution)/shard_map/ppermute | solution.py:433
  14.2 8.0 %collective-permute-start.4 = (f32[240,128]{1,0:T(8,128)}, f32[240,128]{1,0:T(8,128)S(1)}, u32[]{:S(2)}, u32[]{:S(2)}) collective-permute-start(f32[240,128]{1,0:T(8,128)} %get-tuple-element.4.own), channel_id=1, source_target_pairs={{0,3},{1,2},{2,1},{3,0},{4,7},{5,6},{6,5},{7,4},{8,11},{9,10},{10,... | collective-permute-start | bytes 368648 | tf_op jit(solution)/shard_map/ppermute | solution.py:437
  16.7 10.0 %collective-permute-start.3 = (f32[240,128]{1,0:T(8,128)}, f32[240,128]{1,0:T(8,128)S(1)}, u32[]{:S(2)}, u32[]{:S(2)}) collective-permute-start(f32[240,128]{1,0:T(8,128)} %get-tuple-element.4.own), channel_id=1, source_target_pairs={{0,2},{1,3},{2,0},{3,1},{4,6},{5,7},{6,4},{7,5},{8,10},{9,11},{10,... | collective-permute-start | bytes 368648 | tf_op jit(solution)/shard_map/ppermute | solution.py:437
  17.2 9.5 %collective-permute-start.2 = (f32[240,128]{1,0:T(8,128)}, f32[240,128]{1,0:T(8,128)S(1)}, u32[]{:S(2)}, u32[]{:S(2)}) collective-permute-start(f32[240,128]{1,0:T(8,128)} %get-tuple-element.4.own), channel_id=1, source_target_pairs={{0,1},{1,0},{2,3},{3,2},{4,5},{5,4},{6,7},{7,6},{8,9},{9,8},{10,11... | collective-permute-start | bytes 368648 | tf_op jit(solution)/shard_map/ppermute | solution.py:437
  17.5 9.2 %collective-permute-start.5 = (f32[240,128]{1,0:T(8,128)S(1)}, f32[240,128]{1,0:T(8,128)S(1)}, u32[]{:S(2)}, u32[]{:S(2)}) collective-permute-start(f32[240,128]{1,0:T(8,128)S(1)} %get-tuple-element.7), channel_id=1, source_target_pairs={{0,1},{1,0},{2,3},{3,2},{4,5},{5,4},{6,7},{7,6},{8,9},{9,8},{10,11... | collective-permute-start | bytes 368648 | tf_op jit(solution)/shard_map/ppermute | solution.py:437
  18.8 7.9 %collective-permute-start.7 = (f32[240,128]{1,0:T(8,128)S(1)}, f32[240,128]{1,0:T(8,128)S(1)}, u32[]{:S(2)}, u32[]{:S(2)}) collective-permute-start(f32[240,128]{1,0:T(8,128)S(1)} %get-tuple-element.6), channel_id=1, source_target_pairs={{0,3},{1,2},{2,1},{3,0},{4,7},{5,6},{6,5},{7,4},{8,11},{9,10},{10,... | collective-permute-start | bytes 368648 | tf_op jit(solution)/shard_map/ppermute | solution.py:437
  22.3 8.7 %collective-permute-start.6 = (f32[240,128]{1,0:T(8,128)S(1)}, f32[240,128]{1,0:T(8,128)S(1)}, u32[]{:S(2)}, u32[]{:S(2)}) collective-permute-start(f32[240,128]{1,0:T(8,128)S(1)} %get-tuple-element.6), channel_id=1, source_target_pairs={{0,2},{1,3},{2,0},{3,1},{4,6},{5,7},{6,4},{7,5},{8,10},{9,11},{10,... | collective-permute-start | bytes 368648 | tf_op jit(solution)/shard_map/ppermute | solution.py:437
  24.5 6.5 %copy-start = (f32[240,128]{1,0:T(8,128)S(1)}, f32[240,128]{1,0:T(8,128)}, u32[]{:S(2)}) copy-start(f32[240,128]{1,0:T(8,128)} %get-tuple-element.4.own) | copy-start | bytes 368644
  31.0 0.8 %copy-start.1 = (s32[64,128]{1,0:T(8,128)S(1)}, s32[64,128]{1,0:T(8,128)}, u32[]{:S(2)}) copy-start(s32[64,128]{1,0:T(8,128)} %place.1) | copy-start | bytes 98308

commit v2 on v1

v2 whole, which is shorter than its diff:
```python
import jax
import jax.numpy as jnp
import ml_dtypes
import numpy as np
from jax import lax
from jax.experimental import pallas as pl
from jax.experimental.pallas import tpu as pltpu
from jax.sharding import PartitionSpec as P

substep_length = 0.01
AXES = ("dom", "lvl")
SUB, LANE = 8, 128
VALUES = 7
ROWS = VALUES * 32 + 16
COMP = 128
FULL = 3 * COMP
TILES = 5
F32, BF16 = jnp.float32, jnp.bfloat16
WINDOW = ((0, 5, False), (0, 4, True), (0, 4, False), (0, 4, False), (1, 4, False), (1, 3, True), (1, 3, False), (1, 3, False))


def lobatto():
    points = np.array([-1.0, -np.sqrt(3.0 / 7.0), 0.0, np.sqrt(3.0 / 7.0), 1.0])
    weights = np.array([0.1, 49.0 / 90.0, 32.0 / 45.0, 49.0 / 90.0, 0.1])
    factor = np.array(
        [np.prod([points[i] - points[k] for k in range(5) if k != i]) for i in range(5)]
    )
    matrix = np.zeros((5, 5))
    for i in range(5):
        for j in range(5):
            if i == j:
                matrix[i, j] = sum((1.0 / (points[i] - points[k]) for k in range(5) if k != i))
            else:
                matrix[i, j] = factor[i] / (factor[j] * (points[i] - points[j]))
    return matrix, weights


def point_row(a, b, k):
    if a < 4 and b < 4:
        return (k * 16 if k < 4 else 64) + b * 4 + a
    if a < 4:
        return (80 + k * 4 if k < 4 else 120) + a
    if b < 4:
        return 96 + k * 4 + b if k < 4 else 112 + b
    return 116 + k if k < 4 else 124


def element_matrices():
    matrix, weights = lobatto()
    eye = np.eye(5)
    grads = [
        np.einsum("ai,bj,ck->abcijk", *[matrix if x == y else eye for y in range(3)]).reshape(125, 125)
        for x in range(3)
    ]
    cube = np.einsum("a,b,c->abc", weights, weights, weights).reshape(125)
    order = np.array([point_row(a, b, k) for a in range(5) for b in range(5) for k in range(5)])
    both = np.zeros((FULL, 2 * FULL))
    for c in range(3):
        for d in range(3):
            first = grads[c].T @ (cube[:, None] * grads[d])
            shear = grads[d].T @ (cube[:, None] * grads[c])
            if c == d:
                shear = shear + sum(g.T @ (cube[:, None] * g) for g in grads)
            both[np.ix_(c * COMP + order, d * COMP + order)] = first
            both[np.ix_(c * COMP + order, FULL + d * COMP + order)] = shear
    high = both.astype(np.float32).astype(ml_dtypes.bfloat16)
    low = (both - high.astype(np.float64)).astype(np.float32).astype(ml_dtypes.bfloat16)
    return np.concatenate([high, low], axis=0)


def lanes(x, index):
    return jnp.take_along_axis(x, index, axis=1, mode="promise_in_bounds")


def wide(row):
    return jnp.broadcast_to(row, (SUB, LANE))


def as_column(row):
    n = row.shape[1]
    diag = lax.broadcasted_iota(jnp.int32, (n, n), 0) == lax.broadcasted_iota(jnp.int32, (n, n), 1)
    return jnp.sum(jnp.where(diag, jnp.broadcast_to(row, (n, n)), 0.0), axis=1, keepdims=True)


def pack_kernel(u, v, m, lev, lam, mu, conn, own, out, index, stage, aux):
    n = 64
    for i in range(16):
        k, b = i // 4, i % 4
        stage[4 * i : 4 * i + 4, 0:64] = conn[pl.ds(5 * b + k, 4, stride=25), :]
    level = lev[...]
    period = jnp.where(level == 0, 8, jnp.where(level == 1, 4, jnp.where(level == 2, 2, 1)))
    last_corner = conn[100:101, :].astype(F32)
    for i, row in enumerate(
        (conn[0:1, :].astype(F32), conn[4:5, :].astype(F32), conn[20:21, :].astype(F32), last_corner,
         lam[...], mu[...], period.astype(F32))
    ):
        aux[i : i + 1, 0:64] = row
    layer = jnp.where(last_corner >= 4096.0, 1.0, 0.0)
    down = lax.broadcasted_iota(jnp.int32, (n, n), 0)
    across = lax.broadcasted_iota(jnp.int32, (n, n), 1)
    number = down.astype(F32)
    same = (as_column(layer) == layer) & (down < across)
    rank = jnp.sum(jnp.where(same, 1.0, 0.0), axis=0, keepdims=True) + 32.0 * layer
    order = jnp.sum(jnp.where(as_column(rank) == across.astype(F32), number, 0.0), axis=0, keepdims=True)
    order = wide(jnp.concatenate([order, order], axis=1).astype(jnp.int32))
    left = lax.broadcasted_iota(jnp.int32, (SUB, LANE), 1) < 64
    for t in range(4):
        upper = lanes(stage[8 * t : 8 * t + 8, :], order)
        lower = lanes(stage[32 + 8 * t : 40 + 8 * t, :], order)
        index[8 * t : 8 * t + 8, :] = jnp.where(left, upper, lower)
    for t in range(4):
        part = index[8 * t : 8 * t + 8, :]
        high, low = part >> 7, part & 127
        acc = [jnp.zeros((SUB, LANE), F32) for _ in range(VALUES)]
        for r in range(32):
            here = high == r
            for k in range(VALUES):
                if k < 3:
                    row = u[k : k + 1, r * LANE : (r + 1) * LANE]
                elif k < 6:
                    row = v[k - 3 : k - 2, r * LANE : (r + 1) * LANE]
                else:
                    row = m[r : r + 1, :]
                acc[k] = jnp.where(here, lanes(wide(row), low), acc[k])
        for k in range(VALUES):
            out[k * 32 + 8 * t : k * 32 + 8 * t + 8, :] = acc[k]
    out[VALUES * 32 : ROWS, :] = jnp.zeros((16, LANE), F32)
    sorted_aux = lanes(aux[...], order)[:, 0:64]
    corner = {name: sorted_aux[i : i + 1, :] for i, name in enumerate("ozyx")}
    column = {name: as_column(c) for name, c in corner.items()}

    def match(col, row):
        hit = column[col] == corner[row]
        return jnp.sum(jnp.where(hit, number, 0.0), axis=0, keepdims=True)

    slot = jnp.zeros((n, 1), F32)
    for j in range(4):
        count = (lax.broadcasted_iota(jnp.int32, (n, LANE), 1) + (j * LANE + 1)).astype(F32)
        hit = column["o"] == own[j : j + 1, :].astype(F32)
        slot = slot + jnp.sum(jnp.where(hit, count, 0.0), axis=1, keepdims=True)
    slot_row = jnp.sum(jnp.where(down == across, slot, 0.0), axis=0, keepdims=True)
    rows = [
        sorted_aux[4:5, :],
        sorted_aux[5:6, :],
        sorted_aux[6:7, :],
        match("o", "z"),
        match("z", "o"),
        match("o", "y"),
        match("y", "o"),
        match("o", "x"),
        match("x", "o"),
        jnp.where(corner["x"] >= 4096.0, corner["x"] - 4096.0, -1.0),
        jnp.where(slot_row > 0.5, slot_row - 1.0, -2.0),
    ]
    for i, row in enumerate(rows):
        out[VALUES * 32 + i : VALUES * 32 + i + 1, 0:64] = row


def place_kernel(index, place):
    acc = jnp.zeros((64, LANE), F32)
    lane = lax.broadcasted_iota(jnp.int32, (32, LANE), 1).astype(F32)
    sub = lax.broadcasted_iota(jnp.int32, (32, LANE), 0)
    broad = lax.broadcasted_iota(jnp.int32, (LANE, LANE), 0)
    for r in range(32):
        row = index[r : r + 1, :]
        here = sub == (row >> 7)
        left = jnp.concatenate(
            [jnp.where(here, float(r), 0.0), jnp.where(here, lane, 0.0)], axis=0
        ).astype(jnp.bfloat16)
        right = jnp.where(broad == (row & 127), 1.0, 0.0).astype(jnp.bfloat16)
        acc = acc + lax.dot_general(
            left, right, (((1,), (1,)), ((), ())), preferred_element_type=F32
        )
    place[...] = acc.astype(jnp.int32)


def main_kernel(
    flags, own, even, odd, r1, r2, r3, s1, s2, s3, place, matrix, new_u, new_v,
    held, disp, vel, mass, force, high, low, maps, table,
):
    parity, me = flags[0], flags[1]
    lane = lax.broadcasted_iota(jnp.int32, (SUB, LANE), 1)
    sub = lax.broadcasted_iota(jnp.int32, (SUB, LANE), 0)
    left, upper = lane < 64, sub < 4
    is_odd = jnp.full((SUB, LANE), parity, jnp.int32) == 1

    def keep(get, position):
        for r in range(0, ROWS, SUB):
            start = position * ROWS + r
            if not isinstance(start, int):
                start = pl.multiple_of(start, SUB)
            held[pl.ds(start, SUB), :] = get(r)

    keep(lambda r: own[r : r + SUB, :], 4)
    keep(lambda r: jnp.where(is_odd, even[r : r + SUB, :], odd[r : r + SUB, :]), 0)
    keep(lambda r: jnp.where(is_odd, odd[r : r + SUB, :], even[r : r + SUB, :]), 8)
    keep(lambda r: jnp.zeros((SUB, LANE), F32), 9)
    for other, near, cross in ((1, r1, s1), (2, r2, s2), (3, r3, s3)):
        partner = lax.bitwise_xor(me, other)
        away = partner - me
        keep(lambda r, near=near: near[r : r + SUB, :], 4 + away)
        keep(lambda r, cross=cross: cross[r : r + SUB, :], jnp.where(away > 0, away, away + 8))

    step = jnp.float32(substep_length)
    for t in range(TILES):
        for r in range(0, VALUES * 32, SUB):
            x = held[2 * t * ROWS + r : 2 * t * ROWS + r + SUB, :]
            y = held[(2 * t + 1) * ROWS + r : (2 * t + 1) * ROWS + r + SUB, :]
            near = jnp.where(left, x, pltpu.roll(y, 64, 1))
            far = jnp.where(left, pltpu.roll(x, 64, 1), y)
            k, q = r // 32, r % 32
            for p, value in ((q, near), (q + 32, far)):
                if k < 3:
                    row = t * FULL + k * COMP + p
                    disp[row : row + SUB, :] = value
                elif k < 6:
                    row = (t * 3 + k - 3) * 64 + p
                    vel[row : row + SUB, :] = value
                else:
                    row = t * 64 + p
                    mass[row : row + SUB, :] = step * value
        for c in range(3):
            row = t * FULL + c * COMP + 120
            disp[row : row + SUB, :] = jnp.zeros((SUB, LANE), F32)

    def elem(j, i):
        row = j * ROWS + VALUES * 32 + i
        return held[row : row + 1, :]

    ghost = jnp.concatenate([elem(j, 9) for j in range(8)], axis=0)
    corner = jnp.concatenate([elem(j + 1, 10) for j in range(8)], axis=0)
    ghost_t, corner_t = ghost.T, corner.T
    count = lax.broadcasted_iota(jnp.int32, (32, LANE), 0).astype(F32)
    to_next, to_prev = [], []
    for j in range(8):
        hit = corner_t[0:32, j : j + 1] == ghost[j : j + 1, :]
        to_next.append(jnp.sum(jnp.where(hit, count, 0.0), axis=0, keepdims=True))
        hit = ghost_t[32:64, j : j + 1] == corner[j : j + 1, :]
        to_prev.append(jnp.sum(jnp.where(hit, count + 32.0, 0.0), axis=0, keepdims=True))
    none = jnp.zeros((1, LANE), F32)
    to_next += [none, none]
    to_prev = [none] + to_prev + [none]
    half = jnp.where(lane[0:1, :] < 64, 0.0, 64.0)
    first_half = lane[0:1, :] < 64
    layer = (lane[0:1, :] & 63) >= 32

    def join(x, y):
        return jnp.where(first_half, x, pltpu.roll(wide(y), 64, 1)[0:1, :])

    def map_at(t, kind):
        row = (t * 6 + kind) * SUB
        return maps[row : row + SUB, :]

    lame, shear, period = [], [], []
    for t in range(TILES):
        x, y = 2 * t, 2 * t + 1
        lame.append(join(elem(x, 0), elem(y, 0)))
        shear.append(join(elem(x, 1), elem(y, 1)))
        period.append(join(elem(x, 2), elem(y, 2)).astype(jnp.int32))
        rows = [join(elem(x, i), elem(y, i)) + half for i in (3, 4, 5, 6)]
        inside = join(elem(x, 7), elem(y, 7)) + half
        outside = join(to_next[x] + 64.0, to_next[y])
        rows.append(jnp.where(layer, outside, inside))
        inside = join(elem(x, 8), elem(y, 8)) + half
        outside = join(to_prev[x] + 64.0, to_prev[y])
        rows.append(jnp.where(layer, inside, outside))
        for kind, row in enumerate(rows):
            maps[(t * 6 + kind) * SUB : (t * 6 + kind + 1) * SUB, :] = wide(row.astype(jnp.int32))

    def faces(t):
        for c in range(3):
            o = t * FULL + c * COMP
            for r in (0, 8):
                disp[o + 64 + r : o + 72 + r, :] = lanes(disp[o + r : o + r + 8, :], map_at(t, 0))
        for c in range(3):
            o = t * FULL + c * COMP
            for r in (0, 32):
                x = jnp.where(upper, disp[o + r : o + r + 8, :], disp[o + r + 12 : o + r + 20, :])
                to = o + 80 + r // 4
                disp[to : to + 8, :] = lanes(x, map_at(t, 2))
        o = t * FULL
        x = jnp.where(upper, disp[o + 64 : o + 72, :], disp[o + COMP + 60 : o + COMP + 68, :])
        x = lanes(x, map_at(t, 2))
        disp[o + 120 : o + 124, :] = x[0:4, :]
        disp[o + COMP + 120 : o + COMP + 124, :] = x[4:8, :]
        o = o + 2 * COMP
        disp[o + 120 : o + 124, :] = lanes(disp[o + 64 : o + 72, :], map_at(t, 2))[0:4, :]

    def corners(ref, t, row):
        o = t * FULL + row
        x = jnp.where(sub == 1, ref[o + COMP - 1 : o + COMP + 7, :], ref[o + 2 * COMP - 2 : o + 2 * COMP + 6, :])
        return jnp.where(sub == 0, ref[o : o + 8, :], x)

    def ahead(t, following):
        def pick(x, y):
            return lanes(jnp.where(lane < 32, y, x), map_at(t, 4))

        for c in range(3):
            for i in range(3):
                x = disp[pl.ds(t * FULL + c * COMP + 32 * i, SUB, stride=4), :]
                y = disp[pl.ds(following * FULL + c * COMP + 32 * i, SUB, stride=4), :]
                to = t * FULL + c * COMP + 96 + 8 * i
                disp[to : to + 8, :] = pick(x, y)
        x = pick(corners(disp, t, 120), corners(disp, following, 120))
        for c in range(3):
            row = t * FULL + c * COMP + 124
            disp[row : row + 1, :] = x[c : c + 1, :]

    def collect(t, before):
        def pick(x, y):
            return lanes(jnp.where(lane >= 96, y, x), map_at(t, 5))

        for c in range(3):
            for i in range(3):
                row = t * FULL + c * COMP + 96 + 8 * i
                other = before * FULL + c * COMP + 96 + 8 * i
                x = pick(force[row : row + 8, :], force[other : other + 8, :])
                where = pl.ds(t * FULL + c * COMP + 32 * i, SUB, stride=4)
                force[where, :] = force[where, :] + x
        o, w = t * FULL + 120, before * FULL + 120
        mine = jnp.concatenate([force[o + c * COMP + 4 : o + c * COMP + 5, :] for c in range(3)] + [wide(none)[0:5, :]], axis=0)
        theirs = jnp.concatenate([force[w + c * COMP + 4 : w + c * COMP + 5, :] for c in range(3)] + [wide(none)[0:5, :]], axis=0)
        x = pick(mine, theirs)
        for c in range(3):
            row = o + c * COMP
            force[row : row + 1, :] = force[row : row + 1, :] + x[c : c + 1, :]
        for c in range(3):
            o = t * FULL + c * COMP
            for r in (0, 32):
                row = o + 80 + r // 4
                x = lanes(force[row : row + 8, :], map_at(t, 3))
                force[o + r : o + r + 4, :] = force[o + r : o + r + 4, :] + x[0:4, :]
                force[o + r + 16 : o + r + 20, :] = force[o + r + 16 : o + r + 20, :] + x[4:8, :]
            x = lanes(force[o + 120 : o + 128, :], map_at(t, 3))
            force[o + 64 : o + 68, :] = force[o + 64 : o + 68, :] + x[0:4, :]
        for c in range(3):
            o = t * FULL + c * COMP
            for r in range(0, 64, SUB):
                f = force[o + r : o + r + 8, :]
                if r < 16:
                    f = f + lanes(force[o + 64 + r : o + 72 + r, :], map_at(t, 1))
                row = (t * 3 + c) * 64 + r
                speed = vel[row : row + 8, :] - mass[t * 64 + r : t * 64 + r + 8, :] * f
                vel[row : row + 8, :] = speed
                disp[o + r : o + r + 8, :] = disp[o + r : o + r + 8, :] + step * speed

    for s, (begin, end, extra) in enumerate(WINDOW):
        for t in range(begin, end + (1 if extra else 0)):
            faces(t)
        for t in range(begin, end):
            ahead(t, t + 1 if t + 1 < end or extra else t)
            weight = jnp.where((s & (period[t] - 1)) == 0, period[t], 0).astype(F32)
            u = disp[t * FULL : (t + 1) * FULL, :]
            for i, factor in enumerate((lame[t] * weight, shear[t] * weight)):
                x = u * factor
                head = x.astype(BF16)
                high[i * FULL : (i + 1) * FULL, t * LANE : (t + 1) * LANE] = head
                low[i * FULL : (i + 1) * FULL, t * LANE : (t + 1) * LANE] = (x - head.astype(F32)).astype(BF16)
        span = slice(begin * LANE, end * LANE)
        head = high[:, span]
        both = jnp.dot(matrix[...], head, preferred_element_type=F32)
        total = both[0:FULL] + both[FULL:] + jnp.dot(matrix[0:FULL, :], low[:, span], preferred_element_type=F32)
        for t in range(begin, end):
            force[t * FULL : (t + 1) * FULL, :] = total[:, (t - begin) * LANE : (t - begin + 1) * LANE]
        for t in range(begin, end):
            collect(t, t - 1 if t > begin else t)

    for c in range(3):
        for q in range(0, 32, SUB):
            row = 2 * FULL + c * COMP + q
            x, y = disp[row : row + 8, :], disp[row + 32 : row + 40, :]
            table[c * 32 + q : c * 32 + q + 8, :] = jnp.where(left, x, pltpu.roll(y, 64, 1))
            row = (6 + c) * 64 + q
            x, y = vel[row : row + 8, :], vel[row + 32 : row + 40, :]
            table[(3 + c) * 32 + q : (3 + c) * 32 + q + 8, :] = jnp.where(left, x, pltpu.roll(y, 64, 1))
    for t in range(4):
        row, column = place[8 * t : 8 * t + 8, :], place[32 + 8 * t : 32 + 8 * t + 8, :]
        acc = [jnp.zeros((SUB, LANE), F32) for _ in range(6)]
        for q in range(32):
            here = row == q
            for k in range(6):
                value = lanes(wide(table[k * 32 + q : k * 32 + q + 1, :]), column)
                acc[k] = jnp.where(here, value, acc[k])
        for k in range(6):
            for j in range(SUB):
                n = (8 * t + j) * LANE
                ref = new_u if k < 3 else new_v
                ref[k % 3 : k % 3 + 1, n : n + LANE] = acc[k][j : j + 1, :]


VMEM = pl.BlockSpec(memory_space=pltpu.VMEM)
SMEM = pl.BlockSpec(memory_space=pltpu.SMEM)


def main_call():
    return pl.pallas_call(
        main_kernel,
        out_shape=(
            jax.ShapeDtypeStruct((3, 4096), F32),
            jax.ShapeDtypeStruct((3, 4096), F32),
        ),
        in_specs=[SMEM] + [VMEM] * 11,
        out_specs=(VMEM, VMEM),
        scratch_shapes=[
            pltpu.VMEM((10 * ROWS, LANE), F32),
            pltpu.VMEM((TILES * FULL, LANE), F32),
            pltpu.VMEM((TILES * 3 * 64, LANE), F32),
            pltpu.VMEM((TILES * 64, LANE), F32),
            pltpu.VMEM((TILES * FULL, LANE), F32),
            pltpu.VMEM((2 * FULL, TILES * LANE), BF16),
            pltpu.VMEM((2 * FULL, TILES * LANE), BF16),
            pltpu.VMEM((TILES * 6 * SUB, LANE), jnp.int32),
            pltpu.VMEM((6 * 32, LANE), F32),
        ],
        compiler_params=pltpu.CompilerParams(vmem_limit_bytes=40 * 1024 * 1024),
        name="substeps",
    )


def per_device(displacement, velocity, inverse_mass, levels, first_lame, shear_modulus, connectivity, owner_list):
    rows, across = lax.axis_size("dom"), lax.axis_size("lvl")
    block, index = pl.pallas_call(
        pack_kernel,
        out_shape=(
            jax.ShapeDtypeStruct((ROWS, LANE), F32),
            jax.ShapeDtypeStruct((32, LANE), jnp.int32),
        ),
        in_specs=[VMEM] * 8,
        out_specs=(VMEM, VMEM),
        scratch_shapes=[pltpu.VMEM((64, LANE), jnp.int32), pltpu.VMEM((SUB, LANE), F32)],
        name="pack",
    )(
        displacement,
        velocity,
        inverse_mass.reshape(32, LANE),
        levels.reshape(1, 64),
        first_lame.reshape(1, 64),
        shear_modulus.reshape(1, 64),
        connectivity,
        owner_list.reshape(4, LANE),
    )

    def swap_rows(x, shift):
        pairs = []
        for r in range(rows):
            partner = (r ^ 1) if shift == 0 else (((r - 1) ^ 1) + 1) % rows
            pairs += [(r * across + i, partner * across + i) for i in range(across)]
        return lax.ppermute(x, AXES, pairs)

    def swap_near(x, other):
        pairs = [(r * across + i, r * across + (i ^ other)) for r in range(rows) for i in range(across)]
        return lax.ppermute(x, AXES, pairs)

    even = swap_rows(block, 0)
    odd = swap_rows(block, 1)
    near = [swap_near(block, other) for other in (1, 2, 3)]
    place = pl.pallas_call(
        place_kernel,
        out_shape=jax.ShapeDtypeStruct((64, LANE), jnp.int32),
        in_specs=[VMEM],
        out_specs=VMEM,
        name="place",
        cost_estimate=pl.CostEstimate(flops=67_000_000, bytes_accessed=50_000, transcendentals=0),
    )(index)
    parity = lax.axis_index("dom") % 2
    me = lax.axis_index("lvl")
    give_prev_1 = me % 2 == 1
    give_prev_2 = me >= 2
    prev_is_even = parity == 1
    send_1 = jnp.where(give_prev_1 == prev_is_even, even, odd)
    send_2 = jnp.where(give_prev_2 == prev_is_even, even, odd)
    cross = [swap_near(send_1, 1), swap_near(send_2, 2), swap_near(send_2, 3)]
    flags = jnp.stack([parity, me]).astype(jnp.int32)
    return main_call()(flags, block, even, odd, *near, *cross, place, jnp.asarray(element_matrices()))


def solution(mesh):
    both = P(None, AXES)
    flat = P(AXES)
    in_specs = (both, both, flat, flat, flat, flat, both, flat)
    return jax.shard_map(
        per_device, mesh=mesh, in_specs=in_specs, out_specs=(both, both), check_vma=False
    )
```

time: 72.9 us -> 54.9 us (0.75)
  Pallas kernels: 45.9 us -> 25.6 us
  local copies, waits for them, and re-layouts: 2.25 us -> 4.42 us
    pallas_call x1, Pallas kernels: 40.9 us -> 20.2 us  [per_device(): main_call()]
    unnamed x5 -> x7, local copies, waits for them, and re-layouts: 2.25 us -> 4.42 us
  transfers between devices with their start and end apart: 8 -> 8, of which waited for: 2 -> 2; matrix products, arithmetic and copies ran while one was open for 0% -> 0% of each run, Pallas kernels for 3% -> 4%
where the time goes in v2:
time: 54.9 us; the launch traced here: 54.5 us
  Pallas kernels  25.6 us (47%)
  starting transfers between devices  17.9 us (33%)
  waiting for transfers between devices  5.88 us (11%)
  local copies, waits for them, and re-layouts  4.42 us (8%)
  between operations  0.66 us (1%)
    pallas_call x1, Pallas kernels, per_device(): main_call()  20.2 us
    ppermute x2, starting transfers between devices, swap_rows(): return lax.ppermute(x, AXES, pairs)  9.25 us
    ppermute x6, starting transfers between devices, swap_near(): return lax.ppermute(x, AXES, pairs)  8.6 us
    ppermute x6, waiting for transfers between devices, swap_near(): return lax.ppermute(x, AXES, pairs)  5.88 us
    unnamed x7, local copies, waits for them, and re-layouts  4.42 us
    pallas_call x1, Pallas kernels, per_device(): pl.pallas_call(pack_kernel, out_shape=(jax.ShapeDtypeStruct((ROWS, LANE),...  3.24 us
    pallas_call x1, Pallas kernels, per_device(): pl.pallas_call(place_kernel, out_shape=jax.ShapeDtypeStruct((64, LANE), j...  2.12 us
  transfers between devices with their start and end apart: 8, of which 2 were waited for; matrix products, arithmetic and copies ran while one was open for 0% of the time, Pallas kernels for 4%

profile of v2, /device:TPU:1, one launch (start us, length us, event | category | flops | bytes accessed | tf_op | source)
XLA Modules:
  0.0 54.5 jit_solution(60545256567142805)
XLA Ops:
  0.6 1.5 %copy.11.conn = s32[125,64]{1,0:T(8,128)} copy(s32[125,64]{0,1:T(8,128)} %param.15) | data formatting | bytes 64000 | tf_op args[6]
  2.1 3.2 %pack.1 = (f32[240,128]{1,0:T(8,128)}, s32[32,128]{1,0:T(8,128)}) custom-call(f32[3,4096]{1,0:T(4,128)} %u.1, f32[3,4096]{1,0:T(4,128)} %v.1, f32[32,128]{1,0:T(8,128)} %bitcast.7, s32[1,64]{1,0:T(1,128)} %bitcast.9, f32[1,64]{1,0:T(1,128)} %bitcast.10, f32[1,64]{1,0:T(1,128)} %bitcast.11, s32[125,64]{1,0:T(8,128)} %copy.11.conn, s32[4,128]{1,0:T(4,128)} %bitcast.8), custom_call_target="tpu_custom_call" | custom-call | tf_op jit(solution)/shard_map/pack/pallas_call | solution.py:422
  5.4 3.0 %collective-permute-start.1 = (f32[240,128]{1,0:T(8,128)}, f32[240,128]{1,0:T(8,128)S(1)}, u32[]{:S(2)}, u32[]{:S(2)}) collective-permute-start(f32[240,128]{1,0:T(8,128)} %get-tuple-element.4.own), channel_id=1, source_target_pairs={{0,252},{1,253},{2,254},{3,255},{4,8},{5,9},{6,10},{7,11},{8,4},{9... | collective-permute-start | bytes 368648 | tf_op jit(solution)/shard_map/ppermute | solution.py:448
  8.4 6.2 %collective-permute-start = (f32[240,128]{1,0:T(8,128)}, f32[240,128]{1,0:T(8,128)S(1)}, u32[]{:S(2)}, u32[]{:S(2)}) collective-permute-start(f32[240,128]{1,0:T(8,128)} %get-tuple-element.4.own), channel_id=1, source_target_pairs={{0,4},{1,5},{2,6},{3,7},{4,0},{5,1},{6,2},{7,3},{8,12},{9,13},{10,... | collective-permute-start | bytes 368648 | tf_op jit(solution)/shard_map/ppermute | solution.py:448
  14.6 2.5 %collective-permute-start.4 = (f32[240,128]{1,0:T(8,128)}, f32[240,128]{1,0:T(8,128)S(1)}, u32[]{:S(2)}, u32[]{:S(2)}) collective-permute-start(f32[240,128]{1,0:T(8,128)} %get-tuple-element.4.own), channel_id=1, source_target_pairs={{0,3},{1,2},{2,1},{3,0},{4,7},{5,6},{6,5},{7,4},{8,11},{9,10},{10,... | collective-permute-start | bytes 368648 | tf_op jit(solution)/shard_map/ppermute | solution.py:452
  17.1 0.5 collective-permute-start.3
  17.6 0.3 collective-permute-start.2
  17.9 0.0 collective-permute-done.1.odd
  17.9 0.0 collective-permute-done.even
  17.9 1.3 %collective-permute-start.5 = (f32[240,128]{1,0:T(8,128)S(1)}, f32[240,128]{1,0:T(8,128)S(1)}, u32[]{:S(2)}, u32[]{:S(2)}) collective-permute-start(f32[240,128]{1,0:T(8,128)S(1)} %get-tuple-element.7), channel_id=1, source_target_pairs={{0,1},{1,0},{2,3},{3,2},{4,5},{5,4},{6,7},{7,6},{8,9},{9,8},{10,11... | collective-permute-start | bytes 368648 | tf_op jit(solution)/shard_map/ppermute | solution.py:452
  19.2 1.8 %collective-permute-start.7 = (f32[240,128]{1,0:T(8,128)S(1)}, f32[240,128]{1,0:T(8,128)S(1)}, u32[]{:S(2)}, u32[]{:S(2)}) collective-permute-start(f32[240,128]{1,0:T(8,128)S(1)} %get-tuple-element.6), channel_id=1, source_target_pairs={{0,3},{1,2},{2,1},{3,0},{4,7},{5,6},{6,5},{7,4},{8,11},{9,10},{10,... | collective-permute-start | bytes 368648 | tf_op jit(solution)/shard_map/ppermute | solution.py:452
  21.0 1.6 %collective-permute-done.4.r3 = f32[240,128]{1,0:T(8,128)S(1)} collective-permute-done((f32[240,128]{1,0:T(8,128)}, f32[240,128]{1,0:T(8,128)S(1)}, u32[]{:S(2)}, u32[]{:S(2)}) %collective-permute-start.4) | collective-permute-done | bytes 122912 | tf_op jit(solution)/shard_map/ppermute | solution.py:452
  22.6 2.2 %collective-permute-start.6 = (f32[240,128]{1,0:T(8,128)S(1)}, f32[240,128]{1,0:T(8,128)S(1)}, u32[]{:S(2)}, u32[]{:S(2)}) collective-permute-start(f32[240,128]{1,0:T(8,128)S(1)} %get-tuple-element.6), channel_id=1, source_target_pairs={{0,2},{1,3},{2,0},{3,1},{4,6},{5,7},{6,4},{7,5},{8,10},{9,11},{10,... | collective-permute-start | bytes 368648 | tf_op jit(solution)/shard_map/ppermute | solution.py:452
  24.9 2.1 %place.1 = s32[64,128]{1,0:T(8,128)} custom-call(s32[32,128]{1,0:T(8,128)} %get-tuple-element.5.index), custom_call_target="tpu_custom_call" | custom-call | flops 67000000 | bytes 50000 | tf_op jit(solution)/shard_map/place/pallas_call | solution.py:457
  27.0 0.1 pad_add_fusion.flags
  27.1 0.0 collective-permute-done.3.r2
  27.1 0.0 collective-permute-done.2.r1
  27.1 0.0 collective-permute-done.5.s1
  27.1 0.0 collective-permute-done.7.s3
  27.1 4.2 %collective-permute-done.6.s2 = f32[240,128]{1,0:T(8,128)S(1)} collective-permute-done((f32[240,128]{1,0:T(8,128)S(1)}, f32[240,128]{1,0:T(8,128)S(1)}, u32[]{:S(2)}, u32[]{:S(2)}) %collective-permute-start.6) | collective-permute-done | bytes 122912 | tf_op jit(solution)/shard_map/ppermute | solution.py:452
  31.3 1.3 %copy-done = bf16[768,768]{1,0:T(8,128)(2,1)S(1)} copy-done((bf16[768,768]{1,0:T(8,128)(2,1)S(1)}, bf16[768,768]{1,0:T(8,128)(2,1)}, u32[]{:S(2)}) %copy-start) | copy-done | bytes 1179672
  32.6 0.9 %copy-done.1 = f32[240,128]{1,0:T(8,128)S(1)} copy-done((f32[240,128]{1,0:T(8,128)S(1)}, f32[240,128]{1,0:T(8,128)}, u32[]{:S(2)}) %copy-start.1) | copy-done | bytes 122904
  33.5 0.8 %copy-done.2 = s32[64,128]{1,0:T(8,128)S(1)} copy-done((s32[64,128]{1,0:T(8,128)S(1)}, s32[64,128]{1,0:T(8,128)}, u32[]{:S(2)}) %copy-start.2) | copy-done | bytes 32792
  34.3 20.2 %substeps.1 = (f32[3,4096]{1,0:T(4,128)}, f32[3,4096]{1,0:T(4,128)}) custom-call(s32[2]{0:T(128)S(1)} %pad_add_fusion.flags, f32[240,128]{1,0:T(8,128)S(1)} %copy-done.1, f32[240,128]{1,0:T(8,128)S(1)} %collective-permute-done.even, f32[240,128]{1,0:T(8,128)S(1)} %collective-permute-done.1.odd, f32[240,128]{1,0:T(8,128)S(1)} %collective-permute-done.2.r1, ...), custom_call_target="tpu_custom_call" | custom-call | tf_op jit(solution)/shard_map/substeps/pallas_call | solution.py:474
  (4 shorter events, 0.0 us)
Async XLA Ops:
  5.4 12.5 %collective-permute-start.1 = (f32[240,128]{1,0:T(8,128)}, f32[240,128]{1,0:T(8,128)S(1)}, u32[]{:S(2)}, u32[]{:S(2)}) collective-permute-start(f32[240,128]{1,0:T(8,128)} %get-tuple-element.4.own), channel_id=1, source_target_pairs={{0,252},{1,253},{2,254},{3,255},{4,8},{5,9},{6,10},{7,11},{8,4},{9... | collective-permute-start | bytes 368648 | tf_op jit(solution)/shard_map/ppermute | solution.py:448
  8.4 9.5 %collective-permute-start = (f32[240,128]{1,0:T(8,128)}, f32[240,128]{1,0:T(8,128)S(1)}, u32[]{:S(2)}, u32[]{:S(2)}) collective-permute-start(f32[240,128]{1,0:T(8,128)} %get-tuple-element.4.own), channel_id=1, source_target_pairs={{0,4},{1,5},{2,6},{3,7},{4,0},{5,1},{6,2},{7,3},{8,12},{9,13},{10,... | collective-permute-start | bytes 368648 | tf_op jit(solution)/shard_map/ppermute | solution.py:448
  14.6 8.0 %collective-permute-start.4 = (f32[240,128]{1,0:T(8,128)}, f32[240,128]{1,0:T(8,128)S(1)}, u32[]{:S(2)}, u32[]{:S(2)}) collective-permute-start(f32[240,128]{1,0:T(8,128)} %get-tuple-element.4.own), channel_id=1, source_target_pairs={{0,3},{1,2},{2,1},{3,0},{4,7},{5,6},{6,5},{7,4},{8,11},{9,10},{10,... | collective-permute-start | bytes 368648 | tf_op jit(solution)/shard_map/ppermute | solution.py:452
  17.1 10.0 %collective-permute-start.3 = (f32[240,128]{1,0:T(8,128)}, f32[240,128]{1,0:T(8,128)S(1)}, u32[]{:S(2)}, u32[]{:S(2)}) collective-permute-start(f32[240,128]{1,0:T(8,128)} %get-tuple-element.4.own), channel_id=1, source_target_pairs={{0,2},{1,3},{2,0},{3,1},{4,6},{5,7},{6,4},{7,5},{8,10},{9,11},{10,... | collective-permute-start | bytes 368648 | tf_op jit(solution)/shard_map/ppermute | solution.py:452
  17.6 9.5 %collective-permute-start.2 = (f32[240,128]{1,0:T(8,128)}, f32[240,128]{1,0:T(8,128)S(1)}, u32[]{:S(2)}, u32[]{:S(2)}) collective-permute-start(f32[240,128]{1,0:T(8,128)} %get-tuple-element.4.own), channel_id=1, source_target_pairs={{0,1},{1,0},{2,3},{3,2},{4,5},{5,4},{6,7},{7,6},{8,9},{9,8},{10,11... | collective-permute-start | bytes 368648 | tf_op jit(solution)/shard_map/ppermute | solution.py:452
  17.9 9.2 %collective-permute-start.5 = (f32[240,128]{1,0:T(8,128)S(1)}, f32[240,128]{1,0:T(8,128)S(1)}, u32[]{:S(2)}, u32[]{:S(2)}) collective-permute-start(f32[240,128]{1,0:T(8,128)S(1)} %get-tuple-element.7), channel_id=1, source_target_pairs={{0,1},{1,0},{2,3},{3,2},{4,5},{5,4},{6,7},{7,6},{8,9},{9,8},{10,11... | collective-permute-start | bytes 368648 | tf_op jit(solution)/shard_map/ppermute | solution.py:452
  19.2 7.9 %collective-permute-start.7 = (f32[240,128]{1,0:T(8,128)S(1)}, f32[240,128]{1,0:T(8,128)S(1)}, u32[]{:S(2)}, u32[]{:S(2)}) collective-permute-start(f32[240,128]{1,0:T(8,128)S(1)} %get-tuple-element.6), channel_id=1, source_target_pairs={{0,3},{1,2},{2,1},{3,0},{4,7},{5,6},{6,5},{7,4},{8,11},{9,10},{10,... | collective-permute-start | bytes 368648 | tf_op jit(solution)/shard_map/ppermute | solution.py:452
  22.6 8.7 %collective-permute-start.6 = (f32[240,128]{1,0:T(8,128)S(1)}, f32[240,128]{1,0:T(8,128)S(1)}, u32[]{:S(2)}, u32[]{:S(2)}) collective-permute-start(f32[240,128]{1,0:T(8,128)S(1)} %get-tuple-element.6), channel_id=1, source_target_pairs={{0,2},{1,3},{2,0},{3,1},{4,6},{5,7},{6,4},{7,5},{8,10},{9,11},{10,... | collective-permute-start | bytes 368648 | tf_op jit(solution)/shard_map/ppermute | solution.py:452
  31.3 1.3 %copy-start = (bf16[768,768]{1,0:T(8,128)(2,1)S(1)}, bf16[768,768]{1,0:T(8,128)(2,1)}, u32[]{:S(2)}) copy-start(bf16[768,768]{1,0:T(8,128)(2,1)} %constant.29.clone.matrix) | copy-start | bytes 3538948
  32.6 0.9 %copy-start.1 = (f32[240,128]{1,0:T(8,128)S(1)}, f32[240,128]{1,0:T(8,128)}, u32[]{:S(2)}) copy-start(f32[240,128]{1,0:T(8,128)} %get-tuple-element.4.own) | copy-start | bytes 368644
  33.5 0.8 %copy-start.2 = (s32[64,128]{1,0:T(8,128)S(1)}, s32[64,128]{1,0:T(8,128)}, u32[]{:S(2)}) copy-start(s32[64,128]{1,0:T(8,128)} %place.1) | copy-start | bytes 98308

commit v3 on v2

--- a/solution.py
+++ b/solution.py
@@ -82,8 +82,10 @@
     return jnp.sum(jnp.where(diag, jnp.broadcast_to(row, (n, n)), 0.0), axis=1, keepdims=True)
 
 
-def pack_kernel(u, v, m, lev, lam, mu, conn, own, out, index, stage, aux):
+def pack_kernel(u, v, m, lev, lam, mu, stored, own, out, index, stage, aux, turned, conn):
     n = 64
+    turned[:, 0:125] = stored[...].astype(F32)
+    conn[...] = turned[...].T.astype(jnp.int32)
     for i in range(16):
         k, b = i // 4, i % 4
         stage[4 * i : 4 * i + 4, 0:64] = conn[pl.ds(5 * b + k, 4, stride=25), :]
@@ -175,8 +177,8 @@
 
 
 def main_kernel(
-    flags, own, even, odd, r1, r2, r3, s1, s2, s3, place, matrix, new_u, new_v,
-    held, disp, vel, mass, force, high, low, maps, table,
+    flags, own_far, even, odd, r1, r2, r3, s1, s2, s3, place_far, matrix_far, new_u, new_v,
+    held, disp, vel, mass, force, high, low, maps, table, own, place, matrix, sems,
 ):
     parity, me = flags[0], flags[1]
     lane = lax.broadcasted_iota(jnp.int32, (SUB, LANE), 1)
@@ -191,7 +193,12 @@
                 start = pl.multiple_of(start, SUB)
             held[pl.ds(start, SUB), :] = get(r)
 
-    keep(lambda r: own[r : r + SUB, :], 4)
+    copies = [
+        pltpu.make_async_copy(far, near, sems.at[i])
+        for i, (far, near) in enumerate(((own_far, own), (matrix_far, matrix), (place_far, place)))
+    ]
+    for copy in copies:
+        copy.start()
     keep(lambda r: jnp.where(is_odd, even[r : r + SUB, :], odd[r : r + SUB, :]), 0)
     keep(lambda r: jnp.where(is_odd, odd[r : r + SUB, :], even[r : r + SUB, :]), 8)
     keep(lambda r: jnp.zeros((SUB, LANE), F32), 9)
@@ -200,6 +207,8 @@
         away = partner - me
         keep(lambda r, near=near: near[r : r + SUB, :], 4 + away)
         keep(lambda r, cross=cross: cross[r : r + SUB, :], jnp.where(away > 0, away, away + 8))
+    copies[0].wait()
+    keep(lambda r: own[r : r + SUB, :], 4)
 
     step = jnp.float32(substep_length)
     for t in range(TILES):
@@ -344,24 +353,26 @@
                 vel[row : row + 8, :] = speed
                 disp[o + r : o + r + 8, :] = disp[o + r : o + r + 8, :] + step * speed
 
+    copies[1].wait()
     for s, (begin, end, extra) in enumerate(WINDOW):
         for t in range(begin, end + (1 if extra else 0)):
             faces(t)
-        for t in range(begin, end):
-            ahead(t, t + 1 if t + 1 < end or extra else t)
-            weight = jnp.where((s & (period[t] - 1)) == 0, period[t], 0).astype(F32)
-            u = disp[t * FULL : (t + 1) * FULL, :]
-            for i, factor in enumerate((lame[t] * weight, shear[t] * weight)):
-                x = u * factor
-                head = x.astype(BF16)
-                high[i * FULL : (i + 1) * FULL, t * LANE : (t + 1) * LANE] = head
-                low[i * FULL : (i + 1) * FULL, t * LANE : (t + 1) * LANE] = (x - head.astype(F32)).astype(BF16)
-        span = slice(begin * LANE, end * LANE)
-        head = high[:, span]
-        both = jnp.dot(matrix[...], head, preferred_element_type=F32)
-        total = both[0:FULL] + both[FULL:] + jnp.dot(matrix[0:FULL, :], low[:, span], preferred_element_type=F32)
-        for t in range(begin, end):
-            force[t * FULL : (t + 1) * FULL, :] = total[:, (t - begin) * LANE : (t - begin + 1) * LANE]
+        groups = [(g, min(g + 2, end)) for g in range(begin, end, 2)]
+        for first, last_tile in groups:
+            for t in range(first, last_tile):
+                ahead(t, t + 1 if t + 1 < end or extra else t)
+                weight = jnp.where((s & (period[t] - 1)) == 0, period[t], 0).astype(F32)
+                u = disp[t * FULL : (t + 1) * FULL, :]
+                for i, factor in enumerate((lame[t] * weight, shear[t] * weight)):
+                    x = u * factor
+                    head = x.astype(BF16)
+                    high[i * FULL : (i + 1) * FULL, t * LANE : (t + 1) * LANE] = head
+                    low[i * FULL : (i + 1) * FULL, t * LANE : (t + 1) * LANE] = (x - head.astype(F32)).astype(BF16)
+            span = slice(first * LANE, last_tile * LANE)
+            both = jnp.dot(matrix[...], high[:, span], preferred_element_type=F32)
+            total = both[0:FULL] + both[FULL:] + jnp.dot(matrix[0:FULL, :], low[:, span], preferred_element_type=F32)
+            for t in range(first, last_tile):
+                force[t * FULL : (t + 1) * FULL, :] = total[:, (t - first) * LANE : (t - first + 1) * LANE]
         for t in range(begin, end):
             collect(t, t - 1 if t > begin else t)
 
@@ -373,6 +384,7 @@
             row = (6 + c) * 64 + q
             x, y = vel[row : row + 8, :], vel[row + 32 : row + 40, :]
             table[(3 + c) * 32 + q : (3 + c) * 32 + q + 8, :] = jnp.where(left, x, pltpu.roll(y, 64, 1))
+    copies[2].wait()
     for t in range(4):
         row, column = place[8 * t : 8 * t + 8, :], place[32 + 8 * t : 32 + 8 * t + 8, :]
         acc = [jnp.zeros((SUB, LANE), F32) for _ in range(6)]
@@ -390,6 +402,7 @@
 
 VMEM = pl.BlockSpec(memory_space=pltpu.VMEM)
 SMEM = pl.BlockSpec(memory_space=pltpu.SMEM)
+FAR = pl.BlockSpec(memory_space=pltpu.HBM)
 
 
 def main_call():
@@ -399,7 +412,7 @@
             jax.ShapeDtypeStruct((3, 4096), F32),
             jax.ShapeDtypeStruct((3, 4096), F32),
         ),
-        in_specs=[SMEM] + [VMEM] * 11,
+        in_specs=[SMEM, FAR] + [VMEM] * 8 + [FAR, FAR],
         out_specs=(VMEM, VMEM),
         scratch_shapes=[
             pltpu.VMEM((10 * ROWS, LANE), F32),
@@ -411,6 +424,10 @@
             pltpu.VMEM((2 * FULL, TILES * LANE), BF16),
             pltpu.VMEM((TILES * 6 * SUB, LANE), jnp.int32),
             pltpu.VMEM((6 * 32, LANE), F32),
+            pltpu.VMEM((ROWS, LANE), F32),
+            pltpu.VMEM((64, LANE), jnp.int32),
+            pltpu.VMEM((2 * FULL, 2 * FULL), BF16),
+            pltpu.SemaphoreType.DMA((3,)),
         ],
         compiler_params=pltpu.CompilerParams(vmem_limit_bytes=40 * 1024 * 1024),
         name="substeps",
@@ -427,7 +444,8 @@
         ),
         in_specs=[VMEM] * 8,
         out_specs=(VMEM, VMEM),
-        scratch_shapes=[pltpu.VMEM((64, LANE), jnp.int32), pltpu.VMEM((SUB, LANE), F32)],
+        scratch_shapes=[pltpu.VMEM((64, LANE), jnp.int32), pltpu.VMEM((SUB, LANE), F32),
+            pltpu.VMEM((64, LANE), F32), pltpu.VMEM((LANE, 64), jnp.int32)],
         name="pack",
     )(
         displacement,
@@ -436,7 +454,7 @@
         levels.reshape(1, 64),
         first_lame.reshape(1, 64),
         shear_modulus.reshape(1, 64),
-        connectivity,
+        connectivity.T,
         owner_list.reshape(4, LANE),
     )
 
@@ -451,9 +469,11 @@
         pairs = [(r * across + i, r * across + (i ^ other)) for r in range(rows) for i in range(across)]
         return lax.ppermute(x, AXES, pairs)
 
+    near = [swap_near(block, other) for other in (1, 2, 3)]
     even = swap_rows(block, 0)
     odd = swap_rows(block, 1)
-    near = [swap_near(block, other) for other in (1, 2, 3)]
+    matrix = jnp.asarray(element_matrices())
+    odd, even, near, matrix = lax.optimization_barrier((odd, even, near, matrix))
     place = pl.pallas_call(
         place_kernel,
         out_shape=jax.ShapeDtypeStruct((64, LANE), jnp.int32),
@@ -462,6 +482,7 @@
         name="place",
         cost_estimate=pl.CostEstimate(flops=67_000_000, bytes_accessed=50_000, transcendentals=0),
     )(index)
+    even, odd, place = lax.optimization_barrier((even, odd, place))
     parity = lax.axis_index("dom") % 2
     me = lax.axis_index("lvl")
     give_prev_1 = me % 2 == 1
@@ -471,7 +492,8 @@
     send_2 = jnp.where(give_prev_2 == prev_is_even, even, odd)
     cross = [swap_near(send_1, 1), swap_near(send_2, 2), swap_near(send_2, 3)]
     flags = jnp.stack([parity, me]).astype(jnp.int32)
-    return main_call()(flags, block, even, odd, *near, *cross, place, jnp.asarray(element_matrices()))
+    hold = lambda x: pltpu.with_memory_space_constraint(x, pltpu.HBM)
+    return main_call()(flags, hold(block), even, odd, *near, *cross, hold(place), hold(matrix))
 
 
 def solution(mesh):

time: 54.9 us -> 46.7 us (0.85)
  the two profiles are of different devices: /device:TPU:1 before, /device:TPU:2 now
where the time goes in v3:
time: 46.7 us; the launch traced here: 46.5 us
  Pallas kernels  23.4 us (50%)
  starting transfers between devices  16.7 us (36%)
  waiting for transfers between devices  5.55 us (12%)
  between operations  0.82 us (2%)
    pallas_call x1, Pallas kernels, per_device(): main_call()  18 us
    ppermute x6, starting transfers between devices, swap_near(): return lax.ppermute(x, AXES, pairs)  8.52 us
    ppermute x2, starting transfers between devices, swap_rows(): return lax.ppermute(x, AXES, pairs)  8.17 us
    ppermute x6, waiting for transfers between devices, swap_near(): return lax.ppermute(x, AXES, pairs)  4.91 us
    pallas_call x1, Pallas kernels, per_device(): pl.pallas_call(pack_kernel, out_shape=(jax.ShapeDtypeStruct((ROWS, LANE),...  3.29 us
    pallas_call x1, Pallas kernels, per_device(): pl.pallas_call(place_kernel, out_shape=jax.ShapeDtypeStruct((64, LANE), j...  2.11 us
  transfers between devices with their start and end apart: 8, of which 4 were waited for; matrix products, arithmetic and copies ran while one was open for 0% of the time, Pallas kernels for 5%

profile of v3, /device:TPU:2, one launch (start us, length us, event | category | flops | bytes accessed | tf_op | source)
XLA Modules:
  0.0 46.5 jit_solution(16112269917936566080)
XLA Ops:
  0.6 3.3 %pack.1 = (f32[240,128]{1,0:T(8,128)}, s32[32,128]{1,0:T(8,128)}) custom-call(f32[3,4096]{1,0:T(4,128)} %u.1, f32[3,4096]{1,0:T(4,128)} %v.1, f32[32,128]{1,0:T(8,128)} %bitcast.9, s32[1,64]{1,0:T(1,128)} %bitcast.11, f32[1,64]{1,0:T(1,128)} %bitcast.12, f32[1,64]{1,0:T(1,128)} %bitcast.13, s32[64,125]{1,0:T(8,128)} %bitcast.8, s32[4,128]{1,0:T(4,128)} %bitcast.10), custom_call_target="tpu_custom_call" | custom-call | tf_op jit(solution)/shard_map/pack/pallas_call | solution.py:439
  3.9 1.5 %collective-permute-start.4 = (f32[240,128]{1,0:T(8,128)}, f32[240,128]{1,0:T(8,128)S(1)}, u32[]{:S(2)}, u32[]{:S(2)}) collective-permute-start(f32[240,128]{1,0:T(8,128)} %get-tuple-element.13.own_far), channel_id=1, source_target_pairs={{0,3},{1,2},{2,1},{3,0},{4,7},{5,6},{6,5},{7,4},{8,11},{9,10},{10,... | collective-permute-start | bytes 368648 | tf_op jit(solution)/shard_map/ppermute | solution.py:470
  5.4 2.8 %collective-permute-start.3 = (f32[240,128]{1,0:T(8,128)}, f32[240,128]{1,0:T(8,128)S(1)}, u32[]{:S(2)}, u32[]{:S(2)}) collective-permute-start(f32[240,128]{1,0:T(8,128)} %get-tuple-element.13.own_far), channel_id=1, source_target_pairs={{0,2},{1,3},{2,0},{3,1},{4,6},{5,7},{6,4},{7,5},{8,10},{9,11},{10,... | collective-permute-start | bytes 368648 | tf_op jit(solution)/shard_map/ppermute | solution.py:470
  8.3 0.0 collective-permute-start.2
  8.3 0.0 collective-permute-start.1
  8.3 8.2 %collective-permute-start = (f32[240,128]{1,0:T(8,128)}, f32[240,128]{1,0:T(8,128)S(1)}, u32[]{:S(2)}, u32[]{:S(2)}) collective-permute-start(f32[240,128]{1,0:T(8,128)} %get-tuple-element.13.own_far), channel_id=1, source_target_pairs={{0,252},{1,253},{2,254},{3,255},{4,8},{5,9},{6,10},{7,11},{8,4},{9... | collective-permute-start | bytes 368648 | tf_op jit(solution)/shard_map/ppermute | solution.py:466
  16.4 2.1 %place.1.place_far = s32[64,128]{1,0:T(8,128)} custom-call(s32[32,128]{1,0:T(8,128)} %get-tuple-element.16.index), custom_call_target="tpu_custom_call" | custom-call | flops 67000000 | bytes 50000 | tf_op jit(solution)/shard_map/place/pallas_call | solution.py:477
  18.6 0.0 collective-permute-done.4.r3
  18.6 0.0 collective-permute-done.3.r2
  18.6 0.0 collective-permute-done.2.r1
  18.6 0.0 collective-permute-done.1.even
  18.6 0.6 %collective-permute-done.odd = f32[240,128]{1,0:T(8,128)S(1)} collective-permute-done((f32[240,128]{1,0:T(8,128)}, f32[240,128]{1,0:T(8,128)S(1)}, u32[]{:S(2)}, u32[]{:S(2)}) %collective-permute-start) | collective-permute-done | bytes 122912 | tf_op jit(solution)/shard_map/ppermute | solution.py:466
  19.2 0.6 %collective-permute-start.5 = (f32[240,128]{1,0:T(8,128)S(1)}, f32[240,128]{1,0:T(8,128)S(1)}, u32[]{:S(2)}, u32[]{:S(2)}) collective-permute-start(f32[240,128]{1,0:T(8,128)S(1)} %get-tuple-element.25), channel_id=1, source_target_pairs={{0,1},{1,0},{2,3},{3,2},{4,5},{5,4},{6,7},{7,6},{8,9},{9,8},{10,11... | collective-permute-start | bytes 368648 | tf_op jit(solution)/shard_map/ppermute | solution.py:470
  19.9 2.2 %collective-permute-start.7 = (f32[240,128]{1,0:T(8,128)S(1)}, f32[240,128]{1,0:T(8,128)S(1)}, u32[]{:S(2)}, u32[]{:S(2)}) collective-permute-start(f32[240,128]{1,0:T(8,128)S(1)} %get-tuple-element.24), channel_id=1, source_target_pairs={{0,3},{1,2},{2,1},{3,0},{4,7},{5,6},{6,5},{7,4},{8,11},{9,10},{10,... | collective-permute-start | bytes 368648 | tf_op jit(solution)/shard_map/ppermute | solution.py:470
  22.0 1.4 %collective-permute-start.6 = (f32[240,128]{1,0:T(8,128)S(1)}, f32[240,128]{1,0:T(8,128)S(1)}, u32[]{:S(2)}, u32[]{:S(2)}) collective-permute-start(f32[240,128]{1,0:T(8,128)S(1)} %get-tuple-element.24), channel_id=1, source_target_pairs={{0,2},{1,3},{2,0},{3,1},{4,6},{5,7},{6,4},{7,5},{8,10},{9,11},{10,... | collective-permute-start | bytes 368648 | tf_op jit(solution)/shard_map/ppermute | solution.py:470
  23.4 0.1 pad_add_fusion.flags
  23.5 0.7 %collective-permute-done.5.s1 = f32[240,128]{1,0:T(8,128)S(1)} collective-permute-done((f32[240,128]{1,0:T(8,128)S(1)}, f32[240,128]{1,0:T(8,128)S(1)}, u32[]{:S(2)}, u32[]{:S(2)}) %collective-permute-start.5) | collective-permute-done | bytes 122912 | tf_op jit(solution)/shard_map/ppermute | solution.py:470
  24.2 0.7 %collective-permute-done.7.s3 = f32[240,128]{1,0:T(8,128)S(1)} collective-permute-done((f32[240,128]{1,0:T(8,128)S(1)}, f32[240,128]{1,0:T(8,128)S(1)}, u32[]{:S(2)}, u32[]{:S(2)}) %collective-permute-start.7) | collective-permute-done | bytes 122912 | tf_op jit(solution)/shard_map/ppermute | solution.py:470
  24.9 3.5 %collective-permute-done.6.s2 = f32[240,128]{1,0:T(8,128)S(1)} collective-permute-done((f32[240,128]{1,0:T(8,128)S(1)}, f32[240,128]{1,0:T(8,128)S(1)}, u32[]{:S(2)}, u32[]{:S(2)}) %collective-permute-start.6) | collective-permute-done | bytes 122912 | tf_op jit(solution)/shard_map/ppermute | solution.py:470
  28.4 18.0 %substeps.1 = (f32[3,4096]{1,0:T(4,128)}, f32[3,4096]{1,0:T(4,128)}) custom-call(s32[2]{0:T(128)S(1)} %pad_add_fusion.flags, f32[240,128]{1,0:T(8,128)} %get-tuple-element.13.own_far, f32[240,128]{1,0:T(8,128)S(1)} %collective-permute-done.1.even, f32[240,128]{1,0:T(8,128)S(1)} %collective-permute-done.odd, f32[240,128]{1,0:T(8,128)S(1)} %collective-permute-done.2.r1, ...), custom_call_target="tpu_custom_call" | custom-call | tf_op jit(solution)/shard_map/substeps/pallas_call | solution.py:496
  (1 shorter events, 0.0 us)
Async XLA Ops:
  3.9 14.6 %collective-permute-start.4 = (f32[240,128]{1,0:T(8,128)}, f32[240,128]{1,0:T(8,128)S(1)}, u32[]{:S(2)}, u32[]{:S(2)}) collective-permute-start(f32[240,128]{1,0:T(8,128)} %get-tuple-element.13.own_far), channel_id=1, source_target_pairs={{0,3},{1,2},{2,1},{3,0},{4,7},{5,6},{6,5},{7,4},{8,11},{9,10},{10,... | collective-permute-start | bytes 368648 | tf_op jit(solution)/shard_map/ppermute | solution.py:470
  5.4 13.1 %collective-permute-start.3 = (f32[240,128]{1,0:T(8,128)}, f32[240,128]{1,0:T(8,128)S(1)}, u32[]{:S(2)}, u32[]{:S(2)}) collective-permute-start(f32[240,128]{1,0:T(8,128)} %get-tuple-element.13.own_far), channel_id=1, source_target_pairs={{0,2},{1,3},{2,0},{3,1},{4,6},{5,7},{6,4},{7,5},{8,10},{9,11},{10,... | collective-permute-start | bytes 368648 | tf_op jit(solution)/shard_map/ppermute | solution.py:470
  8.3 10.3 %collective-permute-start.2 = (f32[240,128]{1,0:T(8,128)}, f32[240,128]{1,0:T(8,128)S(1)}, u32[]{:S(2)}, u32[]{:S(2)}) collective-permute-start(f32[240,128]{1,0:T(8,128)} %get-tuple-element.13.own_far), channel_id=1, source_target_pairs={{0,1},{1,0},{2,3},{3,2},{4,5},{5,4},{6,7},{7,6},{8,9},{9,8},{10,11... | collective-permute-start | bytes 368648 | tf_op jit(solution)/shard_map/ppermute | solution.py:470
  8.3 10.3 %collective-permute-start.1 = (f32[240,128]{1,0:T(8,128)}, f32[240,128]{1,0:T(8,128)S(1)}, u32[]{:S(2)}, u32[]{:S(2)}) collective-permute-start(f32[240,128]{1,0:T(8,128)} %get-tuple-element.13.own_far), channel_id=1, source_target_pairs={{0,4},{1,5},{2,6},{3,7},{4,0},{5,1},{6,2},{7,3},{8,12},{9,13},{10,... | collective-permute-start | bytes 368648 | tf_op jit(solution)/shard_map/ppermute | solution.py:466
  8.3 10.9 %collective-permute-start = (f32[240,128]{1,0:T(8,128)}, f32[240,128]{1,0:T(8,128)S(1)}, u32[]{:S(2)}, u32[]{:S(2)}) collective-permute-start(f32[240,128]{1,0:T(8,128)} %get-tuple-element.13.own_far), channel_id=1, source_target_pairs={{0,252},{1,253},{2,254},{3,255},{4,8},{5,9},{6,10},{7,11},{8,4},{9... | collective-permute-start | bytes 368648 | tf_op jit(solution)/shard_map/ppermute | solution.py:466
  19.2 5.0 %collective-permute-start.5 = (f32[240,128]{1,0:T(8,128)S(1)}, f32[240,128]{1,0:T(8,128)S(1)}, u32[]{:S(2)}, u32[]{:S(2)}) collective-permute-start(f32[240,128]{1,0:T(8,128)S(1)} %get-tuple-element.25), channel_id=1, source_target_pairs={{0,1},{1,0},{2,3},{3,2},{4,5},{5,4},{6,7},{7,6},{8,9},{9,8},{10,11... | collective-permute-start | bytes 368648 | tf_op jit(solution)/shard_map/ppermute | solution.py:470
  19.9 5.0 %collective-permute-start.7 = (f32[240,128]{1,0:T(8,128)S(1)}, f32[240,128]{1,0:T(8,128)S(1)}, u32[]{:S(2)}, u32[]{:S(2)}) collective-permute-start(f32[240,128]{1,0:T(8,128)S(1)} %get-tuple-element.24), channel_id=1, source_target_pairs={{0,3},{1,2},{2,1},{3,0},{4,7},{5,6},{6,5},{7,4},{8,11},{9,10},{10,... | collective-permute-start | bytes 368648 | tf_op jit(solution)/shard_map/ppermute | solution.py:470
  22.0 6.4 %collective-permute-start.6 = (f32[240,128]{1,0:T(8,128)S(1)}, f32[240,128]{1,0:T(8,128)S(1)}, u32[]{:S(2)}, u32[]{:S(2)}) collective-permute-start(f32[240,128]{1,0:T(8,128)S(1)} %get-tuple-element.24), channel_id=1, source_target_pairs={{0,2},{1,3},{2,0},{3,1},{4,6},{5,7},{6,4},{7,5},{8,10},{9,11},{10,... | collective-permute-start | bytes 368648 | tf_op jit(solution)/shard_map/ppermute | solution.py:470

commit v4 on v3

--- a/solution.py
+++ b/solution.py
@@ -17,6 +17,9 @@
 TILES = 5
 F32, BF16 = jnp.float32, jnp.bfloat16
 WINDOW = ((0, 5, False), (0, 4, True), (0, 4, False), (0, 4, False), (1, 4, False), (1, 3, True), (1, 3, False), (1, 3, False))
+EDGE = (0, 4)
+PLANE = [c * COMP + 4 * i for c in range(3) for i in range(24)] + [c * COMP + 120 for c in range(3)]
+PLANE_ROWS = 80
 
 
 def lobatto():
@@ -65,7 +68,9 @@
             both[np.ix_(c * COMP + order, FULL + d * COMP + order)] = shear
     high = both.astype(np.float32).astype(ml_dtypes.bfloat16)
     low = (both - high.astype(np.float64)).astype(np.float32).astype(ml_dtypes.bfloat16)
-    return np.concatenate([high, low], axis=0)
+    edge = np.zeros((2, PLANE_ROWS, 2 * FULL), high.dtype)
+    edge[0, : len(PLANE)], edge[1, : len(PLANE)] = high[PLANE], low[PLANE]
+    return np.concatenate([high, low, edge[0], edge[1]], axis=0)
 
 
 def lanes(x, index):
@@ -106,12 +111,11 @@
     order = jnp.sum(jnp.where(as_column(rank) == across.astype(F32), number, 0.0), axis=0, keepdims=True)
     order = wide(jnp.concatenate([order, order], axis=1).astype(jnp.int32))
     left = lax.broadcasted_iota(jnp.int32, (SUB, LANE), 1) < 64
+    order_half = order + jnp.where(left, 0, 64)
     for t in range(4):
-        upper = lanes(stage[8 * t : 8 * t + 8, :], order)
-        lower = lanes(stage[32 + 8 * t : 40 + 8 * t, :], order)
-        index[8 * t : 8 * t + 8, :] = jnp.where(left, upper, lower)
-    for t in range(4):
-        part = index[8 * t : 8 * t + 8, :]
+        upper, lower = stage[8 * t : 8 * t + 8, :], stage[32 + 8 * t : 40 + 8 * t, :]
+        part = jnp.where(left, upper, pltpu.roll(lower, 64, 1))
+        index[8 * t : 8 * t + 8, :] = lanes(part, order_half)
         high, low = part >> 7, part & 127
         acc = [jnp.zeros((SUB, LANE), F32) for _ in range(VALUES)]
         for r in range(32):
@@ -125,7 +129,7 @@
                     row = m[r : r + 1, :]
                 acc[k] = jnp.where(here, lanes(wide(row), low), acc[k])
         for k in range(VALUES):
-            out[k * 32 + 8 * t : k * 32 + 8 * t + 8, :] = acc[k]
+            out[k * 32 + 8 * t : k * 32 + 8 * t + 8, :] = lanes(acc[k], order_half)
     out[VALUES * 32 : ROWS, :] = jnp.zeros((16, LANE), F32)
     sorted_aux = lanes(aux[...], order)[:, 0:64]
     corner = {name: sorted_aux[i : i + 1, :] for i, name in enumerate("ozyx")}
@@ -369,7 +373,22 @@
                     high[i * FULL : (i + 1) * FULL, t * LANE : (t + 1) * LANE] = head
                     low[i * FULL : (i + 1) * FULL, t * LANE : (t + 1) * LANE] = (x - head.astype(F32)).astype(BF16)
             span = slice(first * LANE, last_tile * LANE)
-            both = jnp.dot(matrix[...], high[:, span], preferred_element_type=F32)
+            if s in EDGE and last_tile == end:
+                t = first
+                edge = matrix[2 * FULL : 2 * FULL + 2 * PLANE_ROWS, :]
+                both = jnp.dot(edge, high[:, span], preferred_element_type=F32)
+                total = both[0:PLANE_ROWS] + both[PLANE_ROWS:]
+                total = total + jnp.dot(edge[0:PLANE_ROWS], low[:, span], preferred_element_type=F32)
+                for r in range(0, FULL, SUB):
+                    force[t * FULL + r : t * FULL + r + SUB, :] = jnp.zeros((SUB, LANE), F32)
+                for c in range(3):
+                    for i in range(3):
+                        r = c * 24 + 8 * i
+                        force[pl.ds(t * FULL + c * COMP + 32 * i, SUB, stride=4), :] = total[r : r + 8]
+                    row = t * FULL + c * COMP + 120
+                    force[row : row + 1, :] = total[72 + c : 73 + c]
+                continue
+            both = jnp.dot(matrix[0 : 2 * FULL, :], high[:, span], preferred_element_type=F32)
             total = both[0:FULL] + both[FULL:] + jnp.dot(matrix[0:FULL, :], low[:, span], preferred_element_type=F32)
             for t in range(first, last_tile):
                 force[t * FULL : (t + 1) * FULL, :] = total[:, (t - first) * LANE : (t - first + 1) * LANE]
@@ -426,7 +445,7 @@
             pltpu.VMEM((6 * 32, LANE), F32),
             pltpu.VMEM((ROWS, LANE), F32),
             pltpu.VMEM((64, LANE), jnp.int32),
-            pltpu.VMEM((2 * FULL, 2 * FULL), BF16),
+            pltpu.VMEM((2 * FULL + 2 * PLANE_ROWS, 2 * FULL), BF16),
             pltpu.SemaphoreType.DMA((3,)),
         ],
         compiler_params=pltpu.CompilerParams(vmem_limit_bytes=40 * 1024 * 1024),
@@ -473,7 +492,7 @@
     even = swap_rows(block, 0)
     odd = swap_rows(block, 1)
     matrix = jnp.asarray(element_matrices())
-    odd, even, near, matrix = lax.optimization_barrier((odd, even, near, matrix))
+    odd, near[0], even = lax.optimization_barrier((odd, near[0], even))
     place = pl.pallas_call(
         place_kernel,
         out_shape=jax.ShapeDtypeStruct((64, LANE), jnp.int32),
@@ -482,7 +501,6 @@
         name="place",
         cost_estimate=pl.CostEstimate(flops=67_000_000, bytes_accessed=50_000, transcendentals=0),
     )(index)
-    even, odd, place = lax.optimization_barrier((even, odd, place))
     parity = lax.axis_index("dom") % 2
     me = lax.axis_index("lvl")
     give_prev_1 = me % 2 == 1

time: 46.7 us -> 42.9 us (0.919)
  waiting for transfers between devices: 5.55 us -> 2.79 us
  Pallas kernels: 23.4 us -> 22.6 us
    ppermute x6, waiting for transfers between devices: 4.91 us -> 2.79 us  [swap_near(): return lax.ppermute(x, AXES, pairs)]
    ppermute x2, starting transfers between devices: 8.17 us -> 6.41 us  [swap_rows(): return lax.ppermute(x, AXES, pairs)]
    ppermute x6, starting transfers between devices: 8.52 us -> 10 us  [swap_near(): return lax.ppermute(x, AXES, pairs)]
    pallas_call x1, Pallas kernels: 18 us -> 17.3 us  [per_device(): main_call()]
    ppermute x2, waiting for transfers between devices: 0.64 us -> 0.01 us  [swap_rows(): return lax.ppermute(x, AXES, pairs)]
  transfers between devices with their start and end apart: 8 -> 8, of which waited for: 4 -> 2; matrix products, arithmetic and copies ran while one was open for 0% -> 0% of each run, Pallas kernels for 5% -> 5%
where the time goes in v4:
time: 42.9 us; the launch traced here: 42.7 us
  Pallas kernels  22.6 us (53%)
  starting transfers between devices  16.4 us (38%)
  waiting for transfers between devices  2.79 us (7%)
  between operations  0.81 us (2%)
    pallas_call x1, Pallas kernels, per_device(): main_call()  17.3 us
    ppermute x6, starting transfers between devices, swap_near(): return lax.ppermute(x, AXES, pairs)  10 us
    ppermute x2, starting transfers between devices, swap_rows(): return lax.ppermute(x, AXES, pairs)  6.41 us
    pallas_call x1, Pallas kernels, per_device(): pl.pallas_call(pack_kernel, out_shape=(jax.ShapeDtypeStruct((ROWS, LANE),...  3.18 us
    ppermute x6, waiting for transfers between devices, swap_near(): return lax.ppermute(x, AXES, pairs)  2.79 us
    pallas_call x1, Pallas kernels, per_device(): pl.pallas_call(place_kernel, out_shape=jax.ShapeDtypeStruct((64, LANE), j...  2.11 us
  transfers between devices with their start and end apart: 8, of which 2 were waited for; matrix products, arithmetic and copies ran while one was open for 0% of the time, Pallas kernels for 5%

profile of v4, /device:TPU:2, one launch (start us, length us, event | category | flops | bytes accessed | tf_op | source)
XLA Modules:
  0.0 42.7 jit_solution(4284263843582397290)
XLA Ops:
  0.6 3.2 %pack.1 = (f32[240,128]{1,0:T(8,128)}, s32[32,128]{1,0:T(8,128)}) custom-call(f32[3,4096]{1,0:T(4,128)} %u.1, f32[3,4096]{1,0:T(4,128)} %v.1, f32[32,128]{1,0:T(8,128)} %bitcast.9, s32[1,64]{1,0:T(1,128)} %bitcast.11, f32[1,64]{1,0:T(1,128)} %bitcast.12, f32[1,64]{1,0:T(1,128)} %bitcast.13, s32[64,125]{1,0:T(8,128)} %bitcast.8, s32[4,128]{1,0:T(4,128)} %bitcast.10), custom_call_target="tpu_custom_call" | custom-call | tf_op jit(solution)/shard_map/pack/pallas_call | solution.py:458
  3.8 0.0 collective-permute-start.2
  3.8 2.3 %collective-permute-start.1 = (f32[240,128]{1,0:T(8,128)}, f32[240,128]{1,0:T(8,128)S(1)}, u32[]{:S(2)}, u32[]{:S(2)}) collective-permute-start(f32[240,128]{1,0:T(8,128)} %get-tuple-element.7.own_far), channel_id=1, source_target_pairs={{0,1},{1,0},{2,3},{3,2},{4,5},{5,4},{6,7},{7,6},{8,9},{9,8},{10,11... | collective-permute-start | bytes 368648 | tf_op jit(solution)/shard_map/ppermute | solution.py:489
  6.1 6.4 %collective-permute-start = (f32[240,128]{1,0:T(8,128)}, f32[240,128]{1,0:T(8,128)S(1)}, u32[]{:S(2)}, u32[]{:S(2)}) collective-permute-start(f32[240,128]{1,0:T(8,128)} %get-tuple-element.7.own_far), channel_id=1, source_target_pairs={{0,252},{1,253},{2,254},{3,255},{4,8},{5,9},{6,10},{7,11},{8,4},{9... | collective-permute-start | bytes 368648 | tf_op jit(solution)/shard_map/ppermute | solution.py:485
  12.5 2.2 %collective-permute-start.4 = (f32[240,128]{1,0:T(8,128)}, f32[240,128]{1,0:T(8,128)S(1)}, u32[]{:S(2)}, u32[]{:S(2)}) collective-permute-start(f32[240,128]{1,0:T(8,128)} %get-tuple-element.7.own_far), channel_id=1, source_target_pairs={{0,3},{1,2},{2,1},{3,0},{4,7},{5,6},{6,5},{7,4},{8,11},{9,10},{10,... | collective-permute-start | bytes 368648 | tf_op jit(solution)/shard_map/ppermute | solution.py:489
  14.6 1.4 %collective-permute-start.3 = (f32[240,128]{1,0:T(8,128)}, f32[240,128]{1,0:T(8,128)S(1)}, u32[]{:S(2)}, u32[]{:S(2)}) collective-permute-start(f32[240,128]{1,0:T(8,128)} %get-tuple-element.7.own_far), channel_id=1, source_target_pairs={{0,2},{1,3},{2,0},{3,1},{4,6},{5,7},{6,4},{7,5},{8,10},{9,11},{10,... | collective-permute-start | bytes 368648 | tf_op jit(solution)/shard_map/ppermute | solution.py:489
  16.1 0.0 collective-permute-done.2.even
  16.1 0.0 collective-permute-done.1.r1
  16.1 0.0 collective-permute-done.odd
  16.1 0.8 %collective-permute-start.5 = (f32[240,128]{1,0:T(8,128)S(1)}, f32[240,128]{1,0:T(8,128)S(1)}, u32[]{:S(2)}, u32[]{:S(2)}) collective-permute-start(f32[240,128]{1,0:T(8,128)S(1)} %get-tuple-element.13), channel_id=1, source_target_pairs={{0,1},{1,0},{2,3},{3,2},{4,5},{5,4},{6,7},{7,6},{8,9},{9,8},{10,11... | collective-permute-start | bytes 368648 | tf_op jit(solution)/shard_map/ppermute | solution.py:489
  16.9 2.0 %collective-permute-start.7 = (f32[240,128]{1,0:T(8,128)S(1)}, f32[240,128]{1,0:T(8,128)S(1)}, u32[]{:S(2)}, u32[]{:S(2)}) collective-permute-start(f32[240,128]{1,0:T(8,128)S(1)} %get-tuple-element.12), channel_id=1, source_target_pairs={{0,3},{1,2},{2,1},{3,0},{4,7},{5,6},{6,5},{7,4},{8,11},{9,10},{10,... | collective-permute-start | bytes 368648 | tf_op jit(solution)/shard_map/ppermute | solution.py:489
  18.9 1.4 %collective-permute-start.6 = (f32[240,128]{1,0:T(8,128)S(1)}, f32[240,128]{1,0:T(8,128)S(1)}, u32[]{:S(2)}, u32[]{:S(2)}) collective-permute-start(f32[240,128]{1,0:T(8,128)S(1)} %get-tuple-element.12), channel_id=1, source_target_pairs={{0,2},{1,3},{2,0},{3,1},{4,6},{5,7},{6,4},{7,5},{8,10},{9,11},{10,... | collective-permute-start | bytes 368648 | tf_op jit(solution)/shard_map/ppermute | solution.py:489
  20.3 2.1 %place.1.place_far = s32[64,128]{1,0:T(8,128)} custom-call(s32[32,128]{1,0:T(8,128)} %get-tuple-element.11.index), custom_call_target="tpu_custom_call" | custom-call | flops 67000000 | bytes 50000 | tf_op jit(solution)/shard_map/place/pallas_call | solution.py:496
  22.4 0.1 pad_add_fusion.flags
  22.5 0.0 collective-permute-done.4.r3
  22.5 0.0 collective-permute-done.3.r2
  22.5 0.0 collective-permute-done.5.s1
  22.5 0.1 collective-permute-done.7.s3
  22.6 2.7 %collective-permute-done.6.s2 = f32[240,128]{1,0:T(8,128)S(1)} collective-permute-done((f32[240,128]{1,0:T(8,128)S(1)}, f32[240,128]{1,0:T(8,128)S(1)}, u32[]{:S(2)}, u32[]{:S(2)}) %collective-permute-start.6) | collective-permute-done | bytes 122912 | tf_op jit(solution)/shard_map/ppermute | solution.py:489
  25.3 17.3 %substeps.1 = (f32[3,4096]{1,0:T(4,128)}, f32[3,4096]{1,0:T(4,128)}) custom-call(s32[2]{0:T(128)S(1)} %pad_add_fusion.flags, f32[240,128]{1,0:T(8,128)} %get-tuple-element.7.own_far, f32[240,128]{1,0:T(8,128)S(1)} %collective-permute-done.2.even, f32[240,128]{1,0:T(8,128)S(1)} %collective-permute-done.odd, f32[240,128]{1,0:T(8,128)S(1)} %collective-permute-done.1.r1, ...), custom_call_target="tpu_custom_call" | custom-call | tf_op jit(solution)/shard_map/substeps/pallas_call | solution.py:514
  (1 shorter events, 0.0 us)
Async XLA Ops:
  3.8 12.2 %collective-permute-start.2 = (f32[240,128]{1,0:T(8,128)}, f32[240,128]{1,0:T(8,128)S(1)}, u32[]{:S(2)}, u32[]{:S(2)}) collective-permute-start(f32[240,128]{1,0:T(8,128)} %get-tuple-element.7.own_far), channel_id=1, source_target_pairs={{0,4},{1,5},{2,6},{3,7},{4,0},{5,1},{6,2},{7,3},{8,12},{9,13},{10,... | collective-permute-start | bytes 368648 | tf_op jit(solution)/shard_map/ppermute | solution.py:485
  3.8 12.2 %collective-permute-start.1 = (f32[240,128]{1,0:T(8,128)}, f32[240,128]{1,0:T(8,128)S(1)}, u32[]{:S(2)}, u32[]{:S(2)}) collective-permute-start(f32[240,128]{1,0:T(8,128)} %get-tuple-element.7.own_far), channel_id=1, source_target_pairs={{0,1},{1,0},{2,3},{3,2},{4,5},{5,4},{6,7},{7,6},{8,9},{9,8},{10,11... | collective-permute-start | bytes 368648 | tf_op jit(solution)/shard_map/ppermute | solution.py:489
  6.1 10.0 %collective-permute-start = (f32[240,128]{1,0:T(8,128)}, f32[240,128]{1,0:T(8,128)S(1)}, u32[]{:S(2)}, u32[]{:S(2)}) collective-permute-start(f32[240,128]{1,0:T(8,128)} %get-tuple-element.7.own_far), channel_id=1, source_target_pairs={{0,252},{1,253},{2,254},{3,255},{4,8},{5,9},{6,10},{7,11},{8,4},{9... | collective-permute-start | bytes 368648 | tf_op jit(solution)/shard_map/ppermute | solution.py:485
  12.5 10.0 %collective-permute-start.4 = (f32[240,128]{1,0:T(8,128)}, f32[240,128]{1,0:T(8,128)S(1)}, u32[]{:S(2)}, u32[]{:S(2)}) collective-permute-start(f32[240,128]{1,0:T(8,128)} %get-tuple-element.7.own_far), channel_id=1, source_target_pairs={{0,3},{1,2},{2,1},{3,0},{4,7},{5,6},{6,5},{7,4},{8,11},{9,10},{10,... | collective-permute-start | bytes 368648 | tf_op jit(solution)/shard_map/ppermute | solution.py:489
  14.6 7.8 %collective-permute-start.3 = (f32[240,128]{1,0:T(8,128)}, f32[240,128]{1,0:T(8,128)S(1)}, u32[]{:S(2)}, u32[]{:S(2)}) collective-permute-start(f32[240,128]{1,0:T(8,128)} %get-tuple-element.7.own_far), channel_id=1, source_target_pairs={{0,2},{1,3},{2,0},{3,1},{4,6},{5,7},{6,4},{7,5},{8,10},{9,11},{10,... | collective-permute-start | bytes 368648 | tf_op jit(solution)/shard_map/ppermute | solution.py:489
  16.1 6.4 %collective-permute-start.5 = (f32[240,128]{1,0:T(8,128)S(1)}, f32[240,128]{1,0:T(8,128)S(1)}, u32[]{:S(2)}, u32[]{:S(2)}) collective-permute-start(f32[240,128]{1,0:T(8,128)S(1)} %get-tuple-element.13), channel_id=1, source_target_pairs={{0,1},{1,0},{2,3},{3,2},{4,5},{5,4},{6,7},{7,6},{8,9},{9,8},{10,11... | collective-permute-start | bytes 368648 | tf_op jit(solution)/shard_map/ppermute | solution.py:489
  16.9 5.7 %collective-permute-start.7 = (f32[240,128]{1,0:T(8,128)S(1)}, f32[240,128]{1,0:T(8,128)S(1)}, u32[]{:S(2)}, u32[]{:S(2)}) collective-permute-start(f32[240,128]{1,0:T(8,128)S(1)} %get-tuple-element.12), channel_id=1, source_target_pairs={{0,3},{1,2},{2,1},{3,0},{4,7},{5,6},{6,5},{7,4},{8,11},{9,10},{10,... | collective-permute-start | bytes 368648 | tf_op jit(solution)/shard_map/ppermute | solution.py:489
  18.9 6.4 %collective-permute-start.6 = (f32[240,128]{1,0:T(8,128)S(1)}, f32[240,128]{1,0:T(8,128)S(1)}, u32[]{:S(2)}, u32[]{:S(2)}) collective-permute-start(f32[240,128]{1,0:T(8,128)S(1)} %get-tuple-element.12), channel_id=1, source_target_pairs={{0,2},{1,3},{2,0},{3,1},{4,6},{5,7},{6,4},{7,5},{8,10},{9,11},{10,... | collective-permute-start | bytes 368648 | tf_op jit(solution)/shard_map/ppermute | solution.py:489

commit v5 on v4

--- a/solution.py
+++ b/solution.py
@@ -18,6 +18,7 @@
 F32, BF16 = jnp.float32, jnp.bfloat16
 WINDOW = ((0, 5, False), (0, 4, True), (0, 4, False), (0, 4, False), (1, 4, False), (1, 3, True), (1, 3, False), (1, 3, False))
 EDGE = (0, 4)
+DONE = (3, 7)
 PLANE = [c * COMP + 4 * i for c in range(3) for i in range(24)] + [c * COMP + 120 for c in range(3)]
 PLANE_ROWS = 80
 
@@ -392,7 +393,7 @@
             total = both[0:FULL] + both[FULL:] + jnp.dot(matrix[0:FULL, :], low[:, span], preferred_element_type=F32)
             for t in range(first, last_tile):
                 force[t * FULL : (t + 1) * FULL, :] = total[:, (t - first) * LANE : (t - first + 1) * LANE]
-        for t in range(begin, end):
+        for t in range(begin + (1 if s in DONE else 0), end):
             collect(t, t - 1 if t > begin else t)
 
     for c in range(3):

time: 42.9 us -> 42.9 us (level)
  no operation moved by 1% of the time
where the time goes in v5:
time: 42.9 us; the launch traced here: 42.6 us
  Pallas kernels  22.5 us (52%)
  starting transfers between devices  16.4 us (38%)
  waiting for transfers between devices  2.79 us (7%)
  between operations  0.81 us (2%)
    pallas_call x1, Pallas kernels, per_device(): main_call()  17.2 us
    ppermute x6, starting transfers between devices, swap_near(): return lax.ppermute(x, AXES, pairs)  10 us
    ppermute x2, starting transfers between devices, swap_rows(): return lax.ppermute(x, AXES, pairs)  6.41 us
    pallas_call x1, Pallas kernels, per_device(): pl.pallas_call(pack_kernel, out_shape=(jax.ShapeDtypeStruct((ROWS, LANE),...  3.18 us
    ppermute x6, waiting for transfers between devices, swap_near(): return lax.ppermute(x, AXES, pairs)  2.79 us
    pallas_call x1, Pallas kernels, per_device(): pl.pallas_call(place_kernel, out_shape=jax.ShapeDtypeStruct((64, LANE), j...  2.11 us
  transfers between devices with their start and end apart: 8, of which 2 were waited for; matrix products, arithmetic and copies ran while one was open for 0% of the time, Pallas kernels for 5%

profile of v5, /device:TPU:2, one launch (start us, length us, event | category | flops | bytes accessed | tf_op | source)
XLA Modules:
  0.0 42.6 jit_solution(16378578978499986331)
XLA Ops:
  0.6 3.2 %pack.1 = (f32[240,128]{1,0:T(8,128)}, s32[32,128]{1,0:T(8,128)}) custom-call(f32[3,4096]{1,0:T(4,128)} %u.1, f32[3,4096]{1,0:T(4,128)} %v.1, f32[32,128]{1,0:T(8,128)} %bitcast.9, s32[1,64]{1,0:T(1,128)} %bitcast.11, f32[1,64]{1,0:T(1,128)} %bitcast.12, f32[1,64]{1,0:T(1,128)} %bitcast.13, s32[64,125]{1,0:T(8,128)} %bitcast.8, s32[4,128]{1,0:T(4,128)} %bitcast.10), custom_call_target="tpu_custom_call" | custom-call | tf_op jit(solution)/shard_map/pack/pallas_call | solution.py:459
  3.8 0.0 collective-permute-start.2
  3.8 2.3 %collective-permute-start.1 = (f32[240,128]{1,0:T(8,128)}, f32[240,128]{1,0:T(8,128)S(1)}, u32[]{:S(2)}, u32[]{:S(2)}) collective-permute-start(f32[240,128]{1,0:T(8,128)} %get-tuple-element.7.own_far), channel_id=1, source_target_pairs={{0,1},{1,0},{2,3},{3,2},{4,5},{5,4},{6,7},{7,6},{8,9},{9,8},{10,11... | collective-permute-start | bytes 368648 | tf_op jit(solution)/shard_map/ppermute | solution.py:490
  6.1 6.4 %collective-permute-start = (f32[240,128]{1,0:T(8,128)}, f32[240,128]{1,0:T(8,128)S(1)}, u32[]{:S(2)}, u32[]{:S(2)}) collective-permute-start(f32[240,128]{1,0:T(8,128)} %get-tuple-element.7.own_far), channel_id=1, source_target_pairs={{0,252},{1,253},{2,254},{3,255},{4,8},{5,9},{6,10},{7,11},{8,4},{9... | collective-permute-start | bytes 368648 | tf_op jit(solution)/shard_map/ppermute | solution.py:486
  12.5 2.2 %collective-permute-start.4 = (f32[240,128]{1,0:T(8,128)}, f32[240,128]{1,0:T(8,128)S(1)}, u32[]{:S(2)}, u32[]{:S(2)}) collective-permute-start(f32[240,128]{1,0:T(8,128)} %get-tuple-element.7.own_far), channel_id=1, source_target_pairs={{0,3},{1,2},{2,1},{3,0},{4,7},{5,6},{6,5},{7,4},{8,11},{9,10},{10,... | collective-permute-start | bytes 368648 | tf_op jit(solution)/shard_map/ppermute | solution.py:490
  14.6 1.4 %collective-permute-start.3 = (f32[240,128]{1,0:T(8,128)}, f32[240,128]{1,0:T(8,128)S(1)}, u32[]{:S(2)}, u32[]{:S(2)}) collective-permute-start(f32[240,128]{1,0:T(8,128)} %get-tuple-element.7.own_far), channel_id=1, source_target_pairs={{0,2},{1,3},{2,0},{3,1},{4,6},{5,7},{6,4},{7,5},{8,10},{9,11},{10,... | collective-permute-start | bytes 368648 | tf_op jit(solution)/shard_map/ppermute | solution.py:490
  16.1 0.0 collective-permute-done.2.even
  16.1 0.0 collective-permute-done.1.r1
  16.1 0.0 collective-permute-done.odd
  16.1 0.8 %collective-permute-start.5 = (f32[240,128]{1,0:T(8,128)S(1)}, f32[240,128]{1,0:T(8,128)S(1)}, u32[]{:S(2)}, u32[]{:S(2)}) collective-permute-start(f32[240,128]{1,0:T(8,128)S(1)} %get-tuple-element.13), channel_id=1, source_target_pairs={{0,1},{1,0},{2,3},{3,2},{4,5},{5,4},{6,7},{7,6},{8,9},{9,8},{10,11... | collective-permute-start | bytes 368648 | tf_op jit(solution)/shard_map/ppermute | solution.py:490
  16.9 2.0 %collective-permute-start.7 = (f32[240,128]{1,0:T(8,128)S(1)}, f32[240,128]{1,0:T(8,128)S(1)}, u32[]{:S(2)}, u32[]{:S(2)}) collective-permute-start(f32[240,128]{1,0:T(8,128)S(1)} %get-tuple-element.12), channel_id=1, source_target_pairs={{0,3},{1,2},{2,1},{3,0},{4,7},{5,6},{6,5},{7,4},{8,11},{9,10},{10,... | collective-permute-start | bytes 368648 | tf_op jit(solution)/shard_map/ppermute | solution.py:490
  18.9 1.4 %collective-permute-start.6 = (f32[240,128]{1,0:T(8,128)S(1)}, f32[240,128]{1,0:T(8,128)S(1)}, u32[]{:S(2)}, u32[]{:S(2)}) collective-permute-start(f32[240,128]{1,0:T(8,128)S(1)} %get-tuple-element.12), channel_id=1, source_target_pairs={{0,2},{1,3},{2,0},{3,1},{4,6},{5,7},{6,4},{7,5},{8,10},{9,11},{10,... | collective-permute-start | bytes 368648 | tf_op jit(solution)/shard_map/ppermute | solution.py:490
  20.3 2.1 %place.1.place_far = s32[64,128]{1,0:T(8,128)} custom-call(s32[32,128]{1,0:T(8,128)} %get-tuple-element.11.index), custom_call_target="tpu_custom_call" | custom-call | flops 67000000 | bytes 50000 | tf_op jit(solution)/shard_map/place/pallas_call | solution.py:497
  22.4 0.1 pad_add_fusion.flags
  22.5 0.0 collective-permute-done.4.r3
  22.5 0.0 collective-permute-done.3.r2
  22.5 0.0 collective-permute-done.5.s1
  22.5 0.1 collective-permute-done.7.s3
  22.6 2.7 %collective-permute-done.6.s2 = f32[240,128]{1,0:T(8,128)S(1)} collective-permute-done((f32[240,128]{1,0:T(8,128)S(1)}, f32[240,128]{1,0:T(8,128)S(1)}, u32[]{:S(2)}, u32[]{:S(2)}) %collective-permute-start.6) | collective-permute-done | bytes 122912 | tf_op jit(solution)/shard_map/ppermute | solution.py:490
  25.3 17.2 %substeps.1 = (f32[3,4096]{1,0:T(4,128)}, f32[3,4096]{1,0:T(4,128)}) custom-call(s32[2]{0:T(128)S(1)} %pad_add_fusion.flags, f32[240,128]{1,0:T(8,128)} %get-tuple-element.7.own_far, f32[240,128]{1,0:T(8,128)S(1)} %collective-permute-done.2.even, f32[240,128]{1,0:T(8,128)S(1)} %collective-permute-done.odd, f32[240,128]{1,0:T(8,128)S(1)} %collective-permute-done.1.r1, ...), custom_call_target="tpu_custom_call" | custom-call | tf_op jit(solution)/shard_map/substeps/pallas_call | solution.py:515
  (1 shorter events, 0.0 us)
Async XLA Ops:
  3.8 12.2 %collective-permute-start.2 = (f32[240,128]{1,0:T(8,128)}, f32[240,128]{1,0:T(8,128)S(1)}, u32[]{:S(2)}, u32[]{:S(2)}) collective-permute-start(f32[240,128]{1,0:T(8,128)} %get-tuple-element.7.own_far), channel_id=1, source_target_pairs={{0,4},{1,5},{2,6},{3,7},{4,0},{5,1},{6,2},{7,3},{8,12},{9,13},{10,... | collective-permute-start | bytes 368648 | tf_op jit(solution)/shard_map/ppermute | solution.py:486
  3.8 12.2 %collective-permute-start.1 = (f32[240,128]{1,0:T(8,128)}, f32[240,128]{1,0:T(8,128)S(1)}, u32[]{:S(2)}, u32[]{:S(2)}) collective-permute-start(f32[240,128]{1,0:T(8,128)} %get-tuple-element.7.own_far), channel_id=1, source_target_pairs={{0,1},{1,0},{2,3},{3,2},{4,5},{5,4},{6,7},{7,6},{8,9},{9,8},{10,11... | collective-permute-start | bytes 368648 | tf_op jit(solution)/shard_map/ppermute | solution.py:490
  6.1 10.0 %collective-permute-start = (f32[240,128]{1,0:T(8,128)}, f32[240,128]{1,0:T(8,128)S(1)}, u32[]{:S(2)}, u32[]{:S(2)}) collective-permute-start(f32[240,128]{1,0:T(8,128)} %get-tuple-element.7.own_far), channel_id=1, source_target_pairs={{0,252},{1,253},{2,254},{3,255},{4,8},{5,9},{6,10},{7,11},{8,4},{9... | collective-permute-start | bytes 368648 | tf_op jit(solution)/shard_map/ppermute | solution.py:486
  12.5 10.0 %collective-permute-start.4 = (f32[240,128]{1,0:T(8,128)}, f32[240,128]{1,0:T(8,128)S(1)}, u32[]{:S(2)}, u32[]{:S(2)}) collective-permute-start(f32[240,128]{1,0:T(8,128)} %get-tuple-element.7.own_far), channel_id=1, source_target_pairs={{0,3},{1,2},{2,1},{3,0},{4,7},{5,6},{6,5},{7,4},{8,11},{9,10},{10,... | collective-permute-start | bytes 368648 | tf_op jit(solution)/shard_map/ppermute | solution.py:490
  14.6 7.8 %collective-permute-start.3 = (f32[240,128]{1,0:T(8,128)}, f32[240,128]{1,0:T(8,128)S(1)}, u32[]{:S(2)}, u32[]{:S(2)}) collective-permute-start(f32[240,128]{1,0:T(8,128)} %get-tuple-element.7.own_far), channel_id=1, source_target_pairs={{0,2},{1,3},{2,0},{3,1},{4,6},{5,7},{6,4},{7,5},{8,10},{9,11},{10,... | collective-permute-start | bytes 368648 | tf_op jit(solution)/shard_map/ppermute | solution.py:490
  16.1 6.4 %collective-permute-start.5 = (f32[240,128]{1,0:T(8,128)S(1)}, f32[240,128]{1,0:T(8,128)S(1)}, u32[]{:S(2)}, u32[]{:S(2)}) collective-permute-start(f32[240,128]{1,0:T(8,128)S(1)} %get-tuple-element.13), channel_id=1, source_target_pairs={{0,1},{1,0},{2,3},{3,2},{4,5},{5,4},{6,7},{7,6},{8,9},{9,8},{10,11... | collective-permute-start | bytes 368648 | tf_op jit(solution)/shard_map/ppermute | solution.py:490
  16.9 5.7 %collective-permute-start.7 = (f32[240,128]{1,0:T(8,128)S(1)}, f32[240,128]{1,0:T(8,128)S(1)}, u32[]{:S(2)}, u32[]{:S(2)}) collective-permute-start(f32[240,128]{1,0:T(8,128)S(1)} %get-tuple-element.12), channel_id=1, source_target_pairs={{0,3},{1,2},{2,1},{3,0},{4,7},{5,6},{6,5},{7,4},{8,11},{9,10},{10,... | collective-permute-start | bytes 368648 | tf_op jit(solution)/shard_map/ppermute | solution.py:490
  18.9 6.4 %collective-permute-start.6 = (f32[240,128]{1,0:T(8,128)S(1)}, f32[240,128]{1,0:T(8,128)S(1)}, u32[]{:S(2)}, u32[]{:S(2)}) collective-permute-start(f32[240,128]{1,0:T(8,128)S(1)} %get-tuple-element.12), channel_id=1, source_target_pairs={{0,2},{1,3},{2,0},{3,1},{4,6},{5,7},{6,4},{7,5},{8,10},{9,11},{10,... | collective-permute-start | bytes 368648 | tf_op jit(solution)/shard_map/ppermute | solution.py:490

commit v6 on v5

--- a/solution.py
+++ b/solution.py
@@ -510,6 +510,7 @@
     send_1 = jnp.where(give_prev_1 == prev_is_even, even, odd)
     send_2 = jnp.where(give_prev_2 == prev_is_even, even, odd)
     cross = [swap_near(send_1, 1), swap_near(send_2, 2), swap_near(send_2, 3)]
+    near[2], near[1], cross[0], cross[2], cross[1] = lax.optimization_barrier((near[2], near[1], cross[0], cross[2], cross[1]))
     flags = jnp.stack([parity, me]).astype(jnp.int32)
     hold = lambda x: pltpu.with_memory_space_constraint(x, pltpu.HBM)
     return main_call()(flags, hold(block), even, odd, *near, *cross, hold(place), hold(matrix))

time: 42.9 us -> 43 us (level)
  starting transfers between devices: 16.4 us -> 15.6 us
  waiting for transfers between devices: 2.79 us -> 3.36 us
    ppermute x6, starting transfers between devices: 10 us -> 9.21 us  [swap_near(): return lax.ppermute(x, AXES, pairs)]
    ppermute x6, waiting for transfers between devices: 2.79 us -> 3.35 us  [swap_near(): return lax.ppermute(x, AXES, pairs)]
where the time goes in v6:
time: 43 us; the launch traced here: 42.4 us
  Pallas kernels  22.5 us (52%)
  starting transfers between devices  15.6 us (36%)
  waiting for transfers between devices  3.36 us (8%)
  between operations  0.81 us (2%)
    pallas_call x1, Pallas kernels, per_device(): main_call()  17.2 us
    ppermute x6, starting transfers between devices, swap_near(): return lax.ppermute(x, AXES, pairs)  9.21 us
    ppermute x2, starting transfers between devices, swap_rows(): return lax.ppermute(x, AXES, pairs)  6.41 us
    ppermute x6, waiting for transfers between devices, swap_near(): return lax.ppermute(x, AXES, pairs)  3.35 us
    pallas_call x1, Pallas kernels, per_device(): pl.pallas_call(pack_kernel, out_shape=(jax.ShapeDtypeStruct((ROWS, LANE),...  3.18 us
    pallas_call x1, Pallas kernels, per_device(): pl.pallas_call(place_kernel, out_shape=jax.ShapeDtypeStruct((64, LANE), j...  2.11 us
  transfers between devices with their start and end apart: 8, of which 2 were waited for; matrix products, arithmetic and copies ran while one was open for 0% of the time, Pallas kernels for 5%

profile of v6, /device:TPU:2, one launch (start us, length us, event | category | flops | bytes accessed | tf_op | source)
XLA Modules:
  0.0 42.4 jit_solution(8862909129178899678)
XLA Ops:
  0.6 3.2 %pack.1 = (f32[240,128]{1,0:T(8,128)}, s32[32,128]{1,0:T(8,128)}) custom-call(f32[3,4096]{1,0:T(4,128)} %u.1, f32[3,4096]{1,0:T(4,128)} %v.1, f32[32,128]{1,0:T(8,128)} %bitcast.9, s32[1,64]{1,0:T(1,128)} %bitcast.11, f32[1,64]{1,0:T(1,128)} %bitcast.12, f32[1,64]{1,0:T(1,128)} %bitcast.13, s32[64,125]{1,0:T(8,128)} %bitcast.8, s32[4,128]{1,0:T(4,128)} %bitcast.10), custom_call_target="tpu_custom_call" | custom-call | tf_op jit(solution)/shard_map/pack/pallas_call | solution.py:459
  3.8 0.0 collective-permute-start.2
  3.8 2.3 %collective-permute-start.1 = (f32[240,128]{1,0:T(8,128)}, f32[240,128]{1,0:T(8,128)S(1)}, u32[]{:S(2)}, u32[]{:S(2)}) collective-permute-start(f32[240,128]{1,0:T(8,128)} %get-tuple-element.12.own_far), channel_id=1, source_target_pairs={{0,1},{1,0},{2,3},{3,2},{4,5},{5,4},{6,7},{7,6},{8,9},{9,8},{10,11... | collective-permute-start | bytes 368648 | tf_op jit(solution)/shard_map/ppermute | solution.py:490
  6.1 6.4 %collective-permute-start = (f32[240,128]{1,0:T(8,128)}, f32[240,128]{1,0:T(8,128)S(1)}, u32[]{:S(2)}, u32[]{:S(2)}) collective-permute-start(f32[240,128]{1,0:T(8,128)} %get-tuple-element.12.own_far), channel_id=1, source_target_pairs={{0,252},{1,253},{2,254},{3,255},{4,8},{5,9},{6,10},{7,11},{8,4},{9... | collective-permute-start | bytes 368648 | tf_op jit(solution)/shard_map/ppermute | solution.py:486
  12.5 2.4 %collective-permute-start.4 = (f32[240,128]{1,0:T(8,128)}, f32[240,128]{1,0:T(8,128)S(1)}, u32[]{:S(2)}, u32[]{:S(2)}) collective-permute-start(f32[240,128]{1,0:T(8,128)} %get-tuple-element.12.own_far), channel_id=1, source_target_pairs={{0,2},{1,3},{2,0},{3,1},{4,6},{5,7},{6,4},{7,5},{8,10},{9,11},{10,... | collective-permute-start | bytes 368648 | tf_op jit(solution)/shard_map/ppermute | solution.py:490
  14.9 0.5 %collective-permute-start.3 = (f32[240,128]{1,0:T(8,128)}, f32[240,128]{1,0:T(8,128)S(1)}, u32[]{:S(2)}, u32[]{:S(2)}) collective-permute-start(f32[240,128]{1,0:T(8,128)} %get-tuple-element.12.own_far), channel_id=1, source_target_pairs={{0,3},{1,2},{2,1},{3,0},{4,7},{5,6},{6,5},{7,4},{8,11},{9,10},{10,... | collective-permute-start | bytes 368648 | tf_op jit(solution)/shard_map/ppermute | solution.py:490
  15.4 0.0 collective-permute-done.2.even
  15.5 0.0 collective-permute-done.1.r1
  15.5 0.0 collective-permute-done.odd
  15.5 1.8 %collective-permute-start.5 = (f32[240,128]{1,0:T(8,128)S(1)}, f32[240,128]{1,0:T(8,128)S(1)}, u32[]{:S(2)}, u32[]{:S(2)}) collective-permute-start(f32[240,128]{1,0:T(8,128)S(1)} %get-tuple-element.23), channel_id=1, source_target_pairs={{0,1},{1,0},{2,3},{3,2},{4,5},{5,4},{6,7},{7,6},{8,9},{9,8},{10,11... | collective-permute-start | bytes 368648 | tf_op jit(solution)/shard_map/ppermute | solution.py:490
  17.3 1.7 %collective-permute-start.7 = (f32[240,128]{1,0:T(8,128)S(1)}, f32[240,128]{1,0:T(8,128)S(1)}, u32[]{:S(2)}, u32[]{:S(2)}) collective-permute-start(f32[240,128]{1,0:T(8,128)S(1)} %get-tuple-element.22), channel_id=1, source_target_pairs={{0,2},{1,3},{2,0},{3,1},{4,6},{5,7},{6,4},{7,5},{8,10},{9,11},{10,... | collective-permute-start | bytes 368648 | tf_op jit(solution)/shard_map/ppermute | solution.py:490
  19.0 0.5 %collective-permute-start.6 = (f32[240,128]{1,0:T(8,128)S(1)}, f32[240,128]{1,0:T(8,128)S(1)}, u32[]{:S(2)}, u32[]{:S(2)}) collective-permute-start(f32[240,128]{1,0:T(8,128)S(1)} %get-tuple-element.22), channel_id=1, source_target_pairs={{0,3},{1,2},{2,1},{3,0},{4,7},{5,6},{6,5},{7,4},{8,11},{9,10},{10,... | collective-permute-start | bytes 368648 | tf_op jit(solution)/shard_map/ppermute | solution.py:490
  19.5 2.1 %place.1.place_far = s32[64,128]{1,0:T(8,128)} custom-call(s32[32,128]{1,0:T(8,128)} %get-tuple-element.21.index), custom_call_target="tpu_custom_call" | custom-call | flops 67000000 | bytes 50000 | tf_op jit(solution)/shard_map/place/pallas_call | solution.py:497
  21.6 0.1 pad_add_fusion.flags
  21.7 0.0 collective-permute-done.4.r2
  21.7 0.0 collective-permute-done.3.r3
  21.7 0.0 collective-permute-done.5.s1
  21.7 2.1 %collective-permute-done.7.s2 = f32[240,128]{1,0:T(8,128)S(1)} collective-permute-done((f32[240,128]{1,0:T(8,128)S(1)}, f32[240,128]{1,0:T(8,128)S(1)}, u32[]{:S(2)}, u32[]{:S(2)}) %collective-permute-start.7) | collective-permute-done | bytes 122912 | tf_op jit(solution)/shard_map/ppermute | solution.py:490
  23.8 1.2 %collective-permute-done.6.s3 = f32[240,128]{1,0:T(8,128)S(1)} collective-permute-done((f32[240,128]{1,0:T(8,128)S(1)}, f32[240,128]{1,0:T(8,128)S(1)}, u32[]{:S(2)}, u32[]{:S(2)}) %collective-permute-start.6) | collective-permute-done | bytes 122912 | tf_op jit(solution)/shard_map/ppermute | solution.py:490
  25.0 17.2 %substeps.1 = (f32[3,4096]{1,0:T(4,128)}, f32[3,4096]{1,0:T(4,128)}) custom-call(s32[2]{0:T(128)S(1)} %pad_add_fusion.flags, f32[240,128]{1,0:T(8,128)} %get-tuple-element.12.own_far, f32[240,128]{1,0:T(8,128)S(1)} %collective-permute-done.2.even, f32[240,128]{1,0:T(8,128)S(1)} %collective-permute-done.odd, f32[240,128]{1,0:T(8,128)S(1)} %collective-permute-done.1.r1, ...), custom_call_target="tpu_custom_call" | custom-call | tf_op jit(solution)/shard_map/substeps/pallas_call | solution.py:516
  (1 shorter events, 0.0 us)
Async XLA Ops:
  3.8 11.6 %collective-permute-start.2 = (f32[240,128]{1,0:T(8,128)}, f32[240,128]{1,0:T(8,128)S(1)}, u32[]{:S(2)}, u32[]{:S(2)}) collective-permute-start(f32[240,128]{1,0:T(8,128)} %get-tuple-element.12.own_far), channel_id=1, source_target_pairs={{0,4},{1,5},{2,6},{3,7},{4,0},{5,1},{6,2},{7,3},{8,12},{9,13},{10,... | collective-permute-start | bytes 368648 | tf_op jit(solution)/shard_map/ppermute | solution.py:486
  3.8 11.6 %collective-permute-start.1 = (f32[240,128]{1,0:T(8,128)}, f32[240,128]{1,0:T(8,128)S(1)}, u32[]{:S(2)}, u32[]{:S(2)}) collective-permute-start(f32[240,128]{1,0:T(8,128)} %get-tuple-element.12.own_far), channel_id=1, source_target_pairs={{0,1},{1,0},{2,3},{3,2},{4,5},{5,4},{6,7},{7,6},{8,9},{9,8},{10,11... | collective-permute-start | bytes 368648 | tf_op jit(solution)/shard_map/ppermute | solution.py:490
  6.1 9.4 %collective-permute-start = (f32[240,128]{1,0:T(8,128)}, f32[240,128]{1,0:T(8,128)S(1)}, u32[]{:S(2)}, u32[]{:S(2)}) collective-permute-start(f32[240,128]{1,0:T(8,128)} %get-tuple-element.12.own_far), channel_id=1, source_target_pairs={{0,252},{1,253},{2,254},{3,255},{4,8},{5,9},{6,10},{7,11},{8,4},{9... | collective-permute-start | bytes 368648 | tf_op jit(solution)/shard_map/ppermute | solution.py:486
  12.5 9.2 %collective-permute-start.4 = (f32[240,128]{1,0:T(8,128)}, f32[240,128]{1,0:T(8,128)S(1)}, u32[]{:S(2)}, u32[]{:S(2)}) collective-permute-start(f32[240,128]{1,0:T(8,128)} %get-tuple-element.12.own_far), channel_id=1, source_target_pairs={{0,2},{1,3},{2,0},{3,1},{4,6},{5,7},{6,4},{7,5},{8,10},{9,11},{10,... | collective-permute-start | bytes 368648 | tf_op jit(solution)/shard_map/ppermute | solution.py:490
  14.9 6.8 %collective-permute-start.3 = (f32[240,128]{1,0:T(8,128)}, f32[240,128]{1,0:T(8,128)S(1)}, u32[]{:S(2)}, u32[]{:S(2)}) collective-permute-start(f32[240,128]{1,0:T(8,128)} %get-tuple-element.12.own_far), channel_id=1, source_target_pairs={{0,3},{1,2},{2,1},{3,0},{4,7},{5,6},{6,5},{7,4},{8,11},{9,10},{10,... | collective-permute-start | bytes 368648 | tf_op jit(solution)/shard_map/ppermute | solution.py:490
  15.5 6.2 %collective-permute-start.5 = (f32[240,128]{1,0:T(8,128)S(1)}, f32[240,128]{1,0:T(8,128)S(1)}, u32[]{:S(2)}, u32[]{:S(2)}) collective-permute-start(f32[240,128]{1,0:T(8,128)S(1)} %get-tuple-element.23), channel_id=1, source_target_pairs={{0,1},{1,0},{2,3},{3,2},{4,5},{5,4},{6,7},{7,6},{8,9},{9,8},{10,11... | collective-permute-start | bytes 368648 | tf_op jit(solution)/shard_map/ppermute | solution.py:490
  17.3 6.5 %collective-permute-start.7 = (f32[240,128]{1,0:T(8,128)S(1)}, f32[240,128]{1,0:T(8,128)S(1)}, u32[]{:S(2)}, u32[]{:S(2)}) collective-permute-start(f32[240,128]{1,0:T(8,128)S(1)} %get-tuple-element.22), channel_id=1, source_target_pairs={{0,2},{1,3},{2,0},{3,1},{4,6},{5,7},{6,4},{7,5},{8,10},{9,11},{10,... | collective-permute-start | bytes 368648 | tf_op jit(solution)/shard_map/ppermute | solution.py:490
  19.0 6.0 %collective-permute-start.6 = (f32[240,128]{1,0:T(8,128)S(1)}, f32[240,128]{1,0:T(8,128)S(1)}, u32[]{:S(2)}, u32[]{:S(2)}) collective-permute-start(f32[240,128]{1,0:T(8,128)S(1)} %get-tuple-element.22), channel_id=1, source_target_pairs={{0,3},{1,2},{2,1},{3,0},{4,7},{5,6},{6,5},{7,4},{8,11},{9,10},{10,... | collective-permute-start | bytes 368648 | tf_op jit(solution)/shard_map/ppermute | solution.py:490
